TPU v7x, 256 devices: a whole 4x4x8 slice. The times are simulated.
256 devices in a mesh: row: 16 (over z_hi, y, core), col: 16 (over x, z_lo).
Axes of the slice: x: 4, y: 4, z: 8 (z_hi: 2, z_lo: 4; z = z_hi * 4 + z_lo), core: 2. Of those that a mesh axis runs over, the one named last changes fastest.
Arguments:
- coords: float32 [64, 32768], P(None, ('row', 'col')), may hold values from -6 to 6
- dissimilarity: float32 [32768, 16384], P('row', 'col'), as said below
Outputs:
- updated: float32 [64, 32768], P(None, ('row', 'col'))
Inputs may be any that keep to these rules, and one draw needn't show every extreme that they name: `dissimilarity`: each unordered pair of distinct samples appears in exactly one entry, placed as the steps state; the entries that name no pair are positive too.
All inputs are finite; a program needn't handle non-finite values.
Results may differ from a plain program's by a relative error of at most 0.0003.
Values sent between devices are 32-bit elements; how exact they have to be, the bound alone decides.
No kernel may reach another device: no remote copies, remote signals or barrier semaphores. Data moves between devices by JAX's collectives and lax.ppermute only.
A program may use at most 128 MiB of HBM per device.

v0:
```python
import jax
import jax.numpy as jnp
from jax import lax
from jax.sharding import PartitionSpec as P

ITERS = 2


def sent_to_all(x, axis):
    copies = jnp.broadcast_to(x, (lax.axis_size(axis), *x.shape))
    return lax.all_to_all(copies, axis, split_axis=0, concat_axis=0, tiled=True)


def joined_along(parts, dim):
    lengths = list(parts.shape[1:])
    lengths[dim] *= parts.shape[0]
    return jnp.moveaxis(parts, 0, dim).reshape(lengths)


def collect(x, axis, dim):
    parts = sent_to_all(x, axis)
    return joined_along(parts, dim)


def broadcast(x, axis, root):
    return lax.dynamic_index_in_dim(lax.all_gather(x, axis), root, 0, keepdims=False)


def filled_up(lines, length):
    spare = -len(lines) % length
    return jnp.pad(lines, [(0, spare)] + [(0, 0)] * (lines.ndim - 1))


def split_up(x, dim, length):
    before, after = (x.shape[:dim], x.shape[dim + 1 :])
    return jnp.moveaxis(x.reshape(*before, length, -1, *after), dim, 0)


def summed_on_arrival(x, axis, dim):
    parts = split_up(x, dim, lax.axis_size(axis))
    arrived = lax.all_to_all(parts, axis, split_axis=0, concat_axis=0, tiled=True)
    return arrived.sum(axis=0)


def total_of(x, axes):
    lines = x.reshape(-1, x.shape[-1])
    padded = filled_up(lines, lax.axis_size(axes))
    whole = collect(summed_on_arrival(padded, axes, 0), axes, 0)
    return lax.slice_in_dim(whole, 0, len(lines)).reshape(x.shape)


def compute_ratios(values, leading, trailing):
    inner_prod = lax.dot_general(
        leading,
        trailing,
        (((0,), (0,)), ((), ())),
        precision=lax.Precision.HIGHEST,
        preferred_element_type=jnp.float32,
    )
    leading_norms = jnp.sum(leading * leading, axis=0)
    trailing_norms = jnp.sum(trailing * trailing, axis=0)
    spacing = jnp.sqrt(leading_norms[:, None] + trailing_norms[None, :] - 2.0 * inner_prod + 1.0)
    return values / spacing


def pair_terms(leading, trailing, ratios):
    pulled = lax.dot_general(
        trailing,
        ratios,
        (((1,), (1,)), ((), ())),
        precision=lax.Precision.HIGHEST,
        preferred_element_type=jnp.float32,
    )
    pushed = lax.dot_general(
        leading,
        ratios,
        (((1,), (0,)), ((), ())),
        precision=lax.Precision.HIGHEST,
        preferred_element_type=jnp.float32,
    )
    leading_terms = leading * jnp.sum(ratios, axis=1)[None, :] - pulled
    trailing_terms = trailing * jnp.sum(ratios, axis=0)[None, :] - pushed
    return (leading_terms, trailing_terms)


def offdiagonal_terms(values, rows_coords, cols_coords, row_first):
    half_width = values.shape[1]
    leading = jnp.where(row_first, rows_coords, cols_coords)
    partner = jnp.where(row_first, cols_coords, rows_coords)
    offset = jnp.where(row_first, 0, half_width).astype(jnp.int32)
    trailing = lax.dynamic_slice_in_dim(partner, offset, half_width, 1)
    ratios = compute_ratios(values, leading, trailing)
    leading_terms, trailing_terms = pair_terms(leading, trailing, ratios)
    placed = lax.dynamic_update_slice_in_dim(jnp.zeros_like(partner), trailing_terms, offset, 1)
    return (
        jnp.where(row_first, leading_terms, placed),
        jnp.where(row_first, placed, leading_terms),
    )


def diagonal_terms(values, rows_coords, cols_coords, row_first):
    half_width = values.shape[1]
    first_half = rows_coords[:, :half_width]
    second_half = rows_coords[:, half_width:]
    upper_values = values[:half_width]
    lower_values = values[half_width:]
    row_iota = lax.broadcasted_iota(jnp.int32, (half_width, half_width), 0)
    col_iota = lax.broadcasted_iota(jnp.int32, (half_width, half_width), 1)
    cross = compute_ratios(lower_values, second_half, first_half)
    cross_second, cross_first = pair_terms(second_half, first_half, cross)
    early = jnp.where(
        col_iota > row_iota, compute_ratios(upper_values, first_half, first_half), 0.0
    )
    late = jnp.where(
        col_iota < row_iota, compute_ratios(upper_values, second_half, second_half), 0.0
    )
    early_rows, early_cols = pair_terms(first_half, first_half, early)
    late_rows, late_cols = pair_terms(second_half, second_half, late)
    row_share = jnp.concatenate(
        [early_rows + early_cols + cross_first, late_rows + late_cols + cross_second], axis=1
    )
    return (row_share, jnp.zeros_like(row_share))


def tile_terms(values, rows_coords, cols_coords, row_index, col_index):
    return lax.cond(
        row_index == col_index,
        diagonal_terms,
        offdiagonal_terms,
        values,
        rows_coords,
        cols_coords,
        row_index < col_index,
    )


def local(coords, dissimilarity):
    half_width = dissimilarity.shape[1]
    block_width = 2 * half_width
    per_root = lax.axis_size("col") // lax.axis_size("row")
    tile_count = dissimilarity.shape[0] // block_width
    inverse_count = 1.0 / (block_width * lax.axis_size("col"))
    row_pos = lax.axis_index("row")
    col_pos = lax.axis_index("col")
    stacked_tiles = dissimilarity.reshape(tile_count, block_width, half_width)
    slot_indices = jnp.arange(tile_count, dtype=jnp.int32)
    at_root = row_pos == col_pos // per_root
    rows_coords = collect(coords, "col", 1)
    updated = coords
    for iteration in range(ITERS):
        root_piece = rows_coords
        cols_coords = broadcast(root_piece, "row", col_pos // per_root)

        def one_tile(partials, operands):
            row_part, col_part = partials
            values, slot_index = operands
            row_share, col_share = tile_terms(
                values, rows_coords, cols_coords, row_pos * per_root + slot_index, col_pos
            )
            row_part = row_share
            return ((row_part, col_part + col_share), None)

        initial = (jnp.zeros_like(rows_coords), jnp.zeros_like(cols_coords))
        (row_part, col_part), _ = lax.scan(one_tile, initial, (stacked_tiles, slot_indices))
        col_total = total_of(col_part, "row")
        row_part = row_part + jnp.where(at_root, col_total, 0.0)
        updated = summed_on_arrival(row_part, "col", 1) * inverse_count
        if iteration + 1 < ITERS:
            rows_coords = collect(updated, "col", 1)
    return updated


def solution(mesh):
    in_specs = (P(None, ("row", "col")), P("row", "col"))
    out_specs = P(None, ("row", "col"))
    return jax.shard_map(local, mesh=mesh, in_specs=in_specs, out_specs=out_specs, check_vma=False)
```

profile of v0, /device:TPU:6, one launch (start us, length us, event | category | flops | bytes accessed | tf_op | source)
XLA Modules:
  0.0 499.9 jit_solution(5902843282270571865)
XLA Ops:
  6.5 0.0 all-gather.3.cloned.1.call-start
  6.5 0.8 broadcast_in_dim.35
  7.3 22.9 %all_to_all.40 = f32[16,64,128]{2,1,0:T(8,128)S(1)} all-to-all(f32[16,64,128]{2,1,0:T(8,128)S(1)} %broadcast_in_dim.35), channel_id=1, replica_groups=mesh['row'=16,'col'=16] {'col'}, dimensions={0} | all-to-all | bytes 1048576 | tf_op jit(solution)/shard_map/all_to_all | solution.py:11
  30.2 0.3 copy.3
  30.5 0.9 all_gather_reshape.6
  31.4 0.0 all-gather.3.cloned.1.call-update
  31.5 0.0 all-gather.5.cloned.1.call-start
  31.6 108.3 %all-gather.3.cloned.1.call-done = f32[16,64,2048]{2,1,0:T(8,128)} async-done(((f32[1,64,2048]{2,1,0:T(8,128)}), f32[16,64,2048]{2,1,0:T(8,128)}) %all-gather.3.cloned.1.call-update) | async-done | bytes 8388624 | tf_op jit(solution)/shard_map/all_gather | solution.py:26
  139.8 40.7 %conditional.2 = (f32[64,2048]{1,0:T(8,128)S(1)}, f32[64,2048]{1,0:T(8,128)S(1)}) conditional(s32[]{:T(128)} %convert_element_type.6, (pred[]{:T(512)}, f32[16,64,2048]{2,1,0:T(8,128)}, s32[]{:T(128)}, f32[64,2048]{1,0:T(8,128)S(1)}, f32[2048,1024]{1,0:T(8,128)}) %tuple.29, (f32[64,2048]{1,0:T(8,128)S(1)}, f32[2048,1024]{1,0:T(8,128)}) %tuple.30), branch_computations={%region_0.5_spmd, %region_5.14_spmd} | conditional | flops 7275405312 | bytes 84492352 | solution.py:126
  139.8 1.1 multiply_reduce_fusion
  141.0 0.1 multiply_reduce_fusion.1
  141.0 11.8 %fusion.42 = (f32[1024]{0:T(1024)S(1)}, f32[2048]{0:T(1024)S(1)}, f32[2048,1024]{1,0:T(8,128)S(1)}) fusion(f32[2048,1024]{1,0:T(8,128)} %get-tuple-element.109, f32[64,2048]{1,0:T(8,128)S(1)} %get-tuple-element.148, f32[64,1024]{1,0:T(8,128)S(1)} %get-tuple-element.151, f32[1024]{0:T(1024)S(1)} %get-tuple-element.150, f32[2048]{0:T(1024)S(1)} %get-tuple-element.147), kind=kOutput, calls=%fused_computation.98 | convolution fusion | flops 1625289728 | bytes 17588224 | tf_op jit(solution)/shard_map/while/body/eval_jaxpr/cond/branch_0_fun/dot_general | solution.py:53
  152.9 5.2 %fusion = f32[64,2048]{1,0:T(8,128)S(1)} fusion(f32[64,2048]{1,0:T(8,128)S(1)} %broadcast.71, s32[]{:T(128)S(6)} %select_n.83, f32[64,2048]{1,0:T(8,128)S(1)} %get-tuple-element.148, f32[2048,1024]{1,0:T(8,128)S(1)} %get-tuple-element.165, f32[64,1024]{1,0:T(8,128)S(1)} %get-tuple-element.151, f32[1024]{0:T(1024)S(1)} %get-tuple-element.127), kind=kOutput, calls=%fused_computation.3 | convolution fusion | flops 1610743808 | bytes 9441284 | tf_op jit(solution)/shard_map/while/body/eval_jaxpr/cond/branch_0_fun/dot_general | solution.py:74
  158.1 8.2 %broadcast_select_fusion.1 = (f32[64,2048]{1,0:T(8,128)S(1)}, f32[64,2048]{1,0:T(8,128)S(1)}) fusion(f32[64,2048]{1,0:T(8,128)S(1)} %fusion, pred[]{:T(512)} %get-tuple-element.105, f32[64,1024]{1,0:T(8,128)S(1)} %get-tuple-element.151, f32[2048,1024]{1,0:T(8,128)S(1)} %get-tuple-element.165, f32[64,2048]{1,0:T(8,128)S(1)} %get-tuple-element.148, ...), kind=kOutput, calls=%fused_computation.9 | convolution fusion | flops 1611137024 | bytes 10756097 | tf_op jit(solution)/shard_map/while/body/eval_jaxpr/cond/branch_0_fun/dot_general | solution.py:67
  180.5 0.1 reshape.58
  180.7 21.9 %all_to_all.41 = f32[16,4,2048]{2,1,0:T(4,128)S(1)} all-to-all(f32[16,4,2048]{2,1,0:T(4,128)S(1)} %reshape.58), channel_id=1, replica_groups=mesh['row'=16,'col'=16] {'row'}, dimensions={0} | all-to-all | bytes 1048576 | tf_op jit(solution)/shard_map/all_to_all | solution.py:41
  202.5 0.1 reduce_sum.292
  202.6 0.1 broadcast_in_dim.36
  202.7 17.4 %all_to_all.42 = f32[16,4,2048]{2,1,0:T(4,128)S(1)} all-to-all(f32[16,4,2048]{2,1,0:T(4,128)S(1)} %broadcast_in_dim.36), channel_id=1, replica_groups=mesh['row'=16,'col'=16] {'row'}, dimensions={0} | all-to-all | bytes 1048576 | tf_op jit(solution)/shard_map/all_to_all | solution.py:11
  220.1 0.1 broadcast_select_fusion.7
  220.2 0.2 select_n.105
  220.4 0.1 add_bitcast_fusion.1
  220.5 0.1 copy.11
  220.6 0.2 copy.5
  220.8 36.9 %all_to_all.43 = f32[16,64,128]{2,1,0:T(8,128)S(1)} all-to-all(f32[16,64,128]{2,1,0:T(8,128)S(1)} %copy.5), channel_id=1, replica_groups=mesh['row'=16,'col'=16] {'col'}, dimensions={0} | all-to-all | bytes 1048576 | tf_op jit(solution)/shard_map/all_to_all | solution.py:41
  257.8 19.6 %all_to_all.44 = f32[16,64,128]{2,1,0:T(8,128)S(1)} all-to-all(f32[16,64,128]{2,1,0:T(8,128)S(1)} %broadcast_in_dim.38), channel_id=1, replica_groups=mesh['row'=16,'col'=16] {'col'}, dimensions={0} | all-to-all | bytes 1048576 | tf_op jit(solution)/shard_map/all_to_all | solution.py:11
  277.4 0.3 copy.6
  277.7 0.9 all_gather_reshape.7
  278.6 0.0 all-gather.5.cloned.1.call-update
  278.7 104.1 %all-gather.5.cloned.1.call-done = f32[16,64,2048]{2,1,0:T(8,128)} async-done(((f32[1,64,2048]{2,1,0:T(8,128)}), f32[16,64,2048]{2,1,0:T(8,128)}) %all-gather.5.cloned.1.call-update) | async-done | bytes 8388624 | tf_op jit(solution)/shard_map/all_gather | solution.py:26
  382.8 37.5 %conditional.3 = (f32[64,2048]{1,0:T(8,128)S(1)}, f32[64,2048]{1,0:T(8,128)S(1)}) conditional(s32[]{:T(128)} %convert_element_type.6, (pred[]{:T(512)}, f32[16,64,2048]{2,1,0:T(8,128)}, s32[]{:T(128)}, f32[64,2048]{1,0:T(8,128)S(1)}, f32[2048,1024]{1,0:T(8,128)}) %tuple.31, (f32[64,2048]{1,0:T(8,128)S(1)}, f32[2048,1024]{1,0:T(8,128)}) %tuple.32), branch_computations={%region_16.21_spmd, %region_21.30_spmd} | conditional | flops 7275405312 | bytes 84492352 | solution.py:126
  382.8 1.1 multiply_reduce_fusion.4
  383.9 0.1 multiply_reduce_fusion.5
  384.0 12.0 %fusion.46 = (f32[1024]{0:T(1024)S(1)}, f32[2048]{0:T(1024)S(1)}, f32[2048,1024]{1,0:T(8,128)S(1)}) fusion(f32[2048,1024]{1,0:T(8,128)} %get-tuple-element.116, f32[64,2048]{1,0:T(8,128)S(1)} %get-tuple-element.153, f32[64,1024]{1,0:T(8,128)S(1)} %get-tuple-element.156, f32[1024]{0:T(1024)S(1)} %get-tuple-element.155, f32[2048]{0:T(1024)S(1)} %get-tuple-element.152), kind=kOutput, calls=%fused_computation.102 | convolution fusion | flops 1625289728 | bytes 17588224 | tf_op jit(solution)/shard_map/while/body/eval_jaxpr/cond/branch_0_fun/dot_general | solution.py:53
  396.0 5.2 %fusion.21 = f32[64,2048]{1,0:T(8,128)S(1)} fusion(f32[64,2048]{1,0:T(8,128)S(1)} %broadcast.77, s32[]{:T(128)S(6)} %select_n.91, f32[64,2048]{1,0:T(8,128)S(1)} %get-tuple-element.153, f32[2048,1024]{1,0:T(8,128)S(1)} %get-tuple-element.168, f32[64,1024]{1,0:T(8,128)S(1)} %get-tuple-element.156, f32[1024]{0:T(1024)S(1)} %get-tuple-element.137), kind=kOutput, calls=%fused_computation.48 | convolution fusion | flops 1610743808 | bytes 9441284 | tf_op jit(solution)/shard_map/while/body/eval_jaxpr/cond/branch_0_fun/dot_general | solution.py:74
  401.3 8.2 %broadcast_select_fusion.4 = (f32[64,2048]{1,0:T(8,128)S(1)}, f32[64,2048]{1,0:T(8,128)S(1)}) fusion(f32[64,2048]{1,0:T(8,128)S(1)} %fusion.21, pred[]{:T(512)} %get-tuple-element.112, f32[64,1024]{1,0:T(8,128)S(1)} %get-tuple-element.156, f32[2048,1024]{1,0:T(8,128)S(1)} %get-tuple-element.168, f32[64,2048]{1,0:T(8,128)S(1)} %get-tuple-element.153, ...), kind=kOutput, calls=%fused_computation.54 | convolution fusion | flops 1611137024 | bytes 10756097 | tf_op jit(solution)/shard_map/while/body/eval_jaxpr/cond/branch_0_fun/dot_general | solution.py:67
  420.3 0.1 reshape.61
  420.5 17.4 %all_to_all.45 = f32[16,4,2048]{2,1,0:T(4,128)S(1)} all-to-all(f32[16,4,2048]{2,1,0:T(4,128)S(1)} %reshape.61), channel_id=1, replica_groups=mesh['row'=16,'col'=16] {'row'}, dimensions={0} | all-to-all | bytes 1048576 | tf_op jit(solution)/shard_map/all_to_all | solution.py:41
  437.9 0.1 reduce_sum.294
  438.0 0.1 broadcast_in_dim.39
  438.1 17.4 %all_to_all.46 = f32[16,4,2048]{2,1,0:T(4,128)S(1)} all-to-all(f32[16,4,2048]{2,1,0:T(4,128)S(1)} %broadcast_in_dim.39), channel_id=1, replica_groups=mesh['row'=16,'col'=16] {'row'}, dimensions={0} | all-to-all | bytes 1048576 | tf_op jit(solution)/shard_map/all_to_all | solution.py:11
  455.4 0.1 broadcast_select_fusion.6
  455.6 0.2 select_n.107
  455.8 0.1 add_bitcast_fusion
  455.8 0.1 copy.12
  455.9 0.2 copy.8
  456.1 36.0 %all_to_all.47 = f32[16,64,128]{2,1,0:T(8,128)S(1)} all-to-all(f32[16,64,128]{2,1,0:T(8,128)S(1)} %copy.8), channel_id=1, replica_groups=mesh['row'=16,'col'=16] {'col'}, dimensions={0} | all-to-all | bytes 1048576 | tf_op jit(solution)/shard_map/all_to_all | solution.py:41
  492.1 0.6 broadcast_multiply_fusion
  (8 shorter events, 0.3 us)
Async XLA Ops:
  6.5 133.3 %all-gather.3.cloned.1.call-start = ((), (), s32[]{:S(2)}) async-start(), calls=%async_computation.8 | async-start | bytes 8912896 | tf_op jit(solution)/shard_map/all_gather | solution.py:26
  31.5 351.3 %all-gather.5.cloned.1.call-start = ((), (), s32[]{:S(2)}) async-start(), calls=%async_computation.9 | async-start | bytes 8912896 | tf_op jit(solution)/shard_map/all_gather | solution.py:26
Sparse Core Ops, SparseCore 0:
  31.6 108.1 all-gather.2
  278.8 103.9 all-gather.4
where the time goes:
time: 506 us; the launch traced here: 500 us
  waiting for transfers between devices  212 us (42%)
  blocking collectives  189 us (37%)
  matrix products  50.5 us (10%)
  loops' own time  25.2 us (5%)
  between operations  13.8 us (3%)
    all_gather x2, waiting for transfers between devices, broadcast(): lax.all_gather(x, axis)  212 us
    all_to_all x4, blocking collectives, summed_on_arrival(): lax.all_to_all(parts, axis, split_axis=0, concat_axis=0, tiled=True)  112 us
    all_to_all x4, blocking collectives, sent_to_all(): return lax.all_to_all(copies, axis, split_axis=0, concat_axis=0, tiled=True)  77.2 us
    another operation x2, loops' own time, tile_terms(): lax.cond(row_index == col_index, diagonal_terms, offdiagonal_terms, value...  25.2 us
    dot_general x2, matrix products, compute_ratios(): lax.dot_general(leading, trailing, (((0,), (0,)), ((), ())), precision=la...  23.8 us
    dot_general x2, matrix products, pair_terms(): lax.dot_general(trailing, ratios, (((1,), (1,)), ((), ())), precision=lax...  16.3 us
    dot_general x2, matrix products, pair_terms(): lax.dot_general(leading, ratios, (((1,), (0,)), ((), ())), precision=lax....  10.4 us
  transfers between devices with their start and end apart: 2, of which 2 were waited for; matrix products, arithmetic and copies ran while one was open for 0% of the time, Pallas kernels for 0%

commit v1 on v0

v1 whole, which is shorter than its diff:
```python
import jax
import jax.numpy as jnp
from jax import lax
from jax.experimental import pallas as pl
from jax.experimental.pallas import tpu as pltpu
from jax.sharding import PartitionSpec as P

ITERS = 2
DIMS = 64
PIECE = 128
CHUNK = 256
HALF = 4
BLOCK = 8
STACK = 3 * DIMS + 16
SAMPLES = 32768

X_GROUPS = [[z + 4 * x for x in range(4)] for z in range(4)]
Z_GROUPS = [[4 * x + z for z in range(4)] for x in range(4)]
YC_GROUPS = [list(range(8)), list(range(8, 16))]


def nn(a, b):
    return lax.dot_general(a, b, (((1,), (0,)), ((), ())), preferred_element_type=jnp.float32)


def nt(a, b):
    return lax.dot_general(a, b, (((1,), (1,)), ((), ())), preferred_element_type=jnp.float32)


def tile_kernel(where_ref, values_ref, rows_ref, cols_ref, row_out, col_out, left, right, stack, norm_i, norm_j, acc):
    step = pl.program_id(0)
    lead_base, trail_base, diagonal = where_ref[0], where_ref[1], where_ref[2]

    def coords_of(n):
        ref, m = (rows_ref, n) if n < BLOCK else (cols_ref, n - BLOCK)
        return jnp.concatenate([ref[2 * m], ref[2 * m + 1]], axis=1)

    @pl.when(step == 0)
    def _():
        acc[...] = jnp.zeros_like(acc)
        ones = jnp.ones((16, CHUNK), jnp.bfloat16)
        for n in range(2 * BLOCK):
            x = coords_of(n)
            hi = x.astype(jnp.bfloat16)
            rest = x - hi.astype(jnp.float32)
            mid = rest.astype(jnp.bfloat16)
            lo = (rest - mid.astype(jnp.float32)).astype(jnp.bfloat16)
            stack[n] = jnp.concatenate([hi, mid, lo, ones], axis=0)
            right[n] = -2.0 * jnp.concatenate([hi, mid, mid, hi], axis=0)
            hi32, mid32 = hi.astype(jnp.float32), mid.astype(jnp.float32)
            flipped = jnp.concatenate([hi32, mid32], axis=0).T
            flipped16 = flipped.astype(jnp.bfloat16)
            left[n] = jnp.concatenate([flipped16, flipped16], axis=1)
            near = hi32 + mid32
            norm_j[n] = jnp.broadcast_to(jnp.sum(near * near, axis=0, keepdims=True) + 1.0, (8, CHUNK))
            turned = near.T
            norm_i[n] = jnp.broadcast_to(jnp.sum(turned * turned, axis=1, keepdims=True), (CHUNK, PIECE))

    def ratios_of(values, lead, trail):
        inner = nn(left[lead], right[trail])
        ni = norm_i[lead]
        squared = inner + (jnp.concatenate([ni, ni], axis=1) + norm_j[trail, 0:1, :])
        return values * lax.rsqrt(squared)

    def products(ratios, lead, trail):
        hi = ratios.astype(jnp.bfloat16)
        lo = (ratios - hi.astype(jnp.float32)).astype(jnp.bfloat16)
        acc[trail] += nn(stack[lead], hi) + nn(stack[lead], lo)
        return nt(stack[trail], hi) + nt(stack[trail], lo)

    special = jnp.logical_and(diagonal == 1, step < HALF)

    @pl.when(jnp.logical_not(special))
    def _():
        lead = lead_base + step
        pulled = None
        for j in range(HALF):
            trail = trail_base + j
            ratios = ratios_of(values_ref[:, j * CHUNK : (j + 1) * CHUNK], lead, trail)
            part = products(ratios, lead, trail)
            pulled = part if pulled is None else pulled + part
        acc[lead] += pulled

    @pl.when(special)
    def _():
        row_iota = lax.broadcasted_iota(jnp.int32, (CHUNK, CHUNK), 0)
        col_iota = lax.broadcasted_iota(jnp.int32, (CHUNK, CHUNK), 1)
        for j in range(HALF):
            values = values_ref[:, j * CHUNK : (j + 1) * CHUNK]

            @pl.when(step != j)
            def _():
                shift = jnp.where(step > j, HALF, 0)
                lead, trail = step + shift, j + shift
                ratios = ratios_of(values, lead, trail)
                pulled = products(ratios, lead, trail)
                acc[lead] += pulled

            @pl.when(step == j)
            def _():
                for shift, keep in ((0, col_iota > row_iota), (HALF, col_iota < row_iota)):
                    ratios = jnp.where(keep, ratios_of(values, j + shift, j + shift), 0.0)
                    pulled = products(ratios, j + shift, j + shift)
                    acc[j + shift] += pulled

    @pl.when(step == BLOCK - 1)
    def _():
        for n in range(2 * BLOCK):
            x = coords_of(n)
            pulled = acc[n, 0:DIMS] + acc[n, DIMS : 2 * DIMS] + acc[n, 2 * DIMS : 3 * DIMS]
            terms = x * acc[n, 3 * DIMS : 3 * DIMS + 1] - pulled
            out, m = (row_out, n) if n < BLOCK else (col_out, n - BLOCK)
            out[2 * m] = terms[:, :PIECE]
            out[2 * m + 1] = terms[:, PIECE:]


def tile_terms(where, values, rows, cols):
    pieces = jax.ShapeDtypeStruct(rows.shape, jnp.float32)
    whole = pl.BlockSpec(rows.shape, lambda i, w: (0, 0, 0))
    return pl.pallas_call(
        tile_kernel,
        out_shape=(pieces, pieces),
        grid_spec=pltpu.PrefetchScalarGridSpec(
            num_scalar_prefetch=1,
            grid=(BLOCK,),
            in_specs=[pl.BlockSpec((CHUNK, values.shape[1]), lambda i, w: (i, 0)), whole, whole],
            out_specs=(whole, whole),
            scratch_shapes=[
                pltpu.VMEM((2 * BLOCK, CHUNK, CHUNK), jnp.bfloat16),
                pltpu.VMEM((2 * BLOCK, CHUNK, CHUNK), jnp.bfloat16),
                pltpu.VMEM((2 * BLOCK, STACK, CHUNK), jnp.bfloat16),
                pltpu.VMEM((2 * BLOCK, CHUNK, PIECE), jnp.float32),
                pltpu.VMEM((2 * BLOCK, 8, CHUNK), jnp.float32),
                pltpu.VMEM((2 * BLOCK, STACK, CHUNK), jnp.float32),
            ],
        ),
        compiler_params=pltpu.CompilerParams(
            dimension_semantics=("arbitrary",), vmem_limit_bytes=40 * 1024 * 1024
        ),
        cost_estimate=pl.CostEstimate(flops=6_000_000_000, transcendentals=2_097_152, bytes_accessed=10_000_000),
    )(where, values, rows, cols)


def exchange(x, axis, groups):
    return lax.all_to_all(x, axis, split_axis=0, concat_axis=0, tiled=True, axis_index_groups=groups)


def spread(x, axis, groups):
    return exchange(jnp.broadcast_to(x, (len(groups[0]), *x.shape)), axis, groups)


def transposed(x):
    pairs = [(a * 16 + b, b * 16 + a) for a in range(16) for b in range(16)]
    return lax.ppermute(x, ("row", "col"), pairs)


def across(x):
    return lax.ppermute(x, "row", [(a, (a + 8) % 16) for a in range(16)])


def gathered(own, turned, low):
    other = across(turned)
    line = spread(own, "col", Z_GROUPS)
    rows = spread(line, "col", X_GROUPS).reshape(16, DIMS, PIECE)
    both = jnp.stack([jnp.where(low, turned, other), jnp.where(low, other, turned)])
    cols = spread(both, "row", YC_GROUPS)
    return rows, jnp.swapaxes(cols, 0, 1).reshape(16, DIMS, PIECE)


def reduced(row_part, col_part, low):
    halves = jnp.swapaxes(col_part.reshape(2, 8, DIMS, PIECE), 0, 1)
    halves = exchange(halves, "row", YC_GROUPS).sum(axis=0)
    kept = jnp.where(low, halves[0], halves[1])
    sent = jnp.where(low, halves[1], halves[0])
    came = across(sent)
    line = exchange(row_part.reshape(4, 4, DIMS, PIECE), "col", X_GROUPS).sum(axis=0)
    row_sum = exchange(line, "col", Z_GROUPS).sum(axis=0)
    return row_sum, kept + came


def local(coords, dissimilarity):
    row, col = lax.axis_index("row"), lax.axis_index("col")
    low = row < 8
    lead_base = jnp.where(row > col, BLOCK, 0)
    trail_base = jnp.where(row < col, BLOCK, jnp.where(row > col, HALF, 0))
    where = jnp.stack([lead_base, trail_base, (row == col).astype(jnp.int32)]).astype(jnp.int32)
    own, turned = coords, transposed(coords)
    scale = 1.0 / SAMPLES
    for iteration in range(ITERS):
        rows, cols = gathered(own, turned, low)
        row_part, col_part = tile_terms(where, dissimilarity, rows, cols)
        row_sum, col_sum = reduced(row_part, col_part, low)
        if iteration + 1 < ITERS:
            came = transposed(jnp.stack([row_sum, col_sum]))
            own = (row_sum + came[1]) * scale
            turned = (col_sum + came[0]) * scale
        else:
            own = (row_sum + transposed(col_sum)) * scale
    return own


def solution(mesh):
    in_specs = (P(None, ("row", "col")), P("row", "col"))
    out_specs = P(None, ("row", "col"))
    return jax.shard_map(local, mesh=mesh, in_specs=in_specs, out_specs=out_specs, check_vma=False)
```

time: 506 us -> 235 us (0.46)
  waiting for transfers between devices: 212 us -> 66.8 us
  blocking collectives: 189 us -> 51.2 us
  starting transfers between devices: 0.04 us -> 73.3 us
  matrix products: 50.5 us -> 0 us
  Pallas kernels: 0 us -> 29.4 us
  loops' own time: 25.2 us -> 0 us
  between operations: 13.8 us -> 0.23 us
  local copies, waits for them, and re-layouts: 4.84 us -> 10.8 us
    all_gather x2 -> x0, waiting for transfers between devices: 212 us -> none  [broadcast(): lax.all_gather(x, axis)]
    all_to_all x8 -> x4, blocking collectives: 189 us -> 51.2 us  [exchange(): lax.all_to_all(x, axis, split_axis=0, concat_axis=0, tiled=True, axis_ind...]
    dot_general x6 -> x0, matrix products: 50.5 us -> none  [the longest x2 23.8 us: compute_ratios(): lax.dot_general(leading, trailing, (((0,), (0,)), ((), ())), precision=la...]
    all_to_all x0 -> x8, starting transfers between devices: none -> 48.9 us  [exchange(): lax.all_to_all(x, axis, split_axis=0, concat_axis=0, tiled=True, axis_ind...]
    all_to_all x0 -> x8, waiting for transfers between devices: none -> 39.2 us  [exchange(): lax.all_to_all(x, axis, split_axis=0, concat_axis=0, tiled=True, axis_ind...]
    pallas_call x0 -> x2, Pallas kernels: none -> 29.4 us  [tile_terms(): pl.pallas_call(tile_kernel, out_shape=(pieces, pieces), grid_spec=pltpu.P...]
    ppermute x0 -> x7, waiting for transfers between devices: none -> 27.6 us  [the longest x3 23.4 us: transposed(): return lax.ppermute(x, ('row', 'col'), pairs)]
    another operation x2 -> x0, loops' own time: 25.2 us -> none  [tile_terms(): lax.cond(row_index == col_index, diagonal_terms, offdiagonal_terms, value...]
  transfers between devices with their start and end apart: 2 -> 15, of which waited for: 2 -> 12; matrix products, arithmetic and copies ran while one was open for 0% -> 2% of each run, Pallas kernels for 0% -> 0%
where the time goes in v1:
time: 235 us; the launch traced here: 234 us
  starting transfers between devices  73.3 us (31%)
  waiting for transfers between devices  66.8 us (28%)
  blocking collectives  51.2 us (22%)
  Pallas kernels  29.4 us (13%)
  local copies, waits for them, and re-layouts  10.8 us (5%)
    all_to_all x4, blocking collectives, exchange(): lax.all_to_all(x, axis, split_axis=0, concat_axis=0, tiled=True, axis_ind...  51.2 us
    all_to_all x8, starting transfers between devices, exchange(): lax.all_to_all(x, axis, split_axis=0, concat_axis=0, tiled=True, axis_ind...  48.9 us
    all_to_all x8, waiting for transfers between devices, exchange(): lax.all_to_all(x, axis, split_axis=0, concat_axis=0, tiled=True, axis_ind...  39.2 us
    pallas_call x2, Pallas kernels, tile_terms(): pl.pallas_call(tile_kernel, out_shape=(pieces, pieces), grid_spec=pltpu.P...  29.4 us
    ppermute x3, waiting for transfers between devices, transposed(): return lax.ppermute(x, ('row', 'col'), pairs)  23.4 us
    ppermute x3, starting transfers between devices, transposed(): return lax.ppermute(x, ('row', 'col'), pairs)  20 us
    unnamed x4, local copies, waits for them, and re-layouts  6.76 us
  transfers between devices with their start and end apart: 15, of which 12 were waited for; matrix products, arithmetic and copies ran while one was open for 2% of the time, Pallas kernels for 0%

profile of v1, /device:TPU:6, one launch (start us, length us, event | category | flops | bytes accessed | tf_op | source)
XLA Modules:
  0.0 233.8 jit_solution(15081152733640753150)
XLA Ops:
  0.0 11.6 %collective-permute-start = (f32[64,128]{1,0:T(8,128)}, f32[64,128]{1,0:T(8,128)S(1)}, u32[]{:S(2)}, u32[]{:S(2)}) collective-permute-start(f32[64,128]{1,0:T(8,128)} %param.2), channel_id=1, source_target_pairs={{0,0},{1,16},{2,32},{3,48},{4,64},{5,80},{6,96},{7,112},{8,128},{9... | collective-permute-start | bytes 98312 | tf_op jit(solution)/shard_map/ppermute | solution.py:154
  11.6 3.0 %collective-permute-done = f32[64,128]{1,0:T(8,128)S(1)} collective-permute-done((f32[64,128]{1,0:T(8,128)}, f32[64,128]{1,0:T(8,128)S(1)}, u32[]{:S(2)}, u32[]{:S(2)}) %collective-permute-start) | collective-permute-done | bytes 32800 | tf_op jit(solution)/shard_map/ppermute | solution.py:154
  14.7 0.9 collective-permute-start.1
  15.6 1.4 broadcast_in_dim.18
  17.0 5.2 %all-to-all-start = ((f32[4,64,128]{2,1,0:T(8,128)}), f32[4,64,128]{2,1,0:T(8,128)S(1)}, u32[]{:S(2)}, u32[]{:S(2)}) async-start(f32[4,64,128]{2,1,0:T(8,128)} %broadcast_in_dim.18), calls=%async_computation | async-start | bytes 262144 | tf_op jit(solution)/shard_map/all_to_all | solution.py:145
  22.3 0.3 collective-permute-done.1
  22.6 5.6 %all-to-all-done = f32[4,64,128]{2,1,0:T(8,128)S(1)} async-done(((f32[4,64,128]{2,1,0:T(8,128)}), f32[4,64,128]{2,1,0:T(8,128)S(1)}, u32[]{:S(2)}, u32[]{:S(2)}) %all-to-all-start) | async-done | bytes 131104 | tf_op jit(solution)/shard_map/all_to_all | solution.py:145
  28.2 12.8 %all_to_all.60 = f32[8,2,64,128]{3,2,1,0:T(8,128)S(1)} all-to-all(f32[8,2,64,128]{3,2,1,0:T(8,128)S(1)} %broadcast_in_dim.20), channel_id=1, replica_groups={{0,16,32,48,64,80,96,112},{128,144,160,176,192,208,224,240},{1,17,33,49..., dimensions={0} | all-to-all | bytes 1048576 | tf_op jit(solution)/shard_map/all_to_all | solution.py:145
  41.0 0.9 broadcast_in_dim.19
  41.9 9.8 %all-to-all-start.1 = ((f32[4,4,64,128]{3,2,1,0:T(8,128)}), f32[4,4,64,128]{3,2,1,0:T(8,128)S(1)}, u32[]{:S(2)}, u32[]{:S(2)}) async-start(f32[4,4,64,128]{3,2,1,0:T(8,128)} %broadcast_in_dim.19), calls=%async_computation.1 | async-start | bytes 1048576 | tf_op jit(solution)/shard_map/all_to_all | solution.py:145
  51.7 0.1 pad_add_fusion.where_ref
  51.9 7.2 %all-to-all-done.1 = f32[4,4,64,128]{3,2,1,0:T(8,128)S(1)} async-done(((f32[4,4,64,128]{3,2,1,0:T(8,128)}), f32[4,4,64,128]{3,2,1,0:T(8,128)S(1)}, u32[]{:S(2)}, u32[]{:S(2)}) %all-to-all-start.1) | async-done | bytes 524320 | tf_op jit(solution)/shard_map/all_to_all | solution.py:145
  59.1 0.0 copy-start
  59.1 3.4 %copy-done = f32[2048,1024]{1,0:T(8,128)S(1)} copy-done((f32[2048,1024]{1,0:T(8,128)S(1)}, f32[2048,1024]{1,0:T(8,128)}, u32[]{:S(2)}) %copy-start) | copy-done | bytes 8388632
  62.4 14.7 %shard_map.28 = (f32[16,64,128]{2,1,0:T(8,128)}, f32[16,64,128]{2,1,0:T(8,128)S(1)}) custom-call(s32[3]{0:T(128)S(1)} %pad_add_fusion.where_ref, f32[2048,1024]{1,0:T(8,128)S(1)} %copy-done, f32[16,64,128]{2,1,0:T(8,128)S(1)} %bitcast.49, f32[16,64,128]{2,1,0:T(8,128)S(1)} %bitcast.52), custom_call_target="tpu_custom_call" | custom-call | flops 6000000000 | bytes 10000000 | tf_op jit(solution)/shard_map/pallas_call | solution.py:120
  77.2 12.8 %all_to_all.61 = f32[8,2,64,128]{3,2,1,0:T(8,128)S(1)} all-to-all(f32[8,2,64,128]{3,2,1,0:T(8,128)S(1)} %bitcast.57), channel_id=1, replica_groups={{0,16,32,48,64,80,96,112},{128,144,160,176,192,208,224,240},{1,17,33,49..., dimensions={0} | all-to-all | bytes 1048576 | tf_op jit(solution)/shard_map/all_to_all | solution.py:145
  90.0 9.2 %all-to-all-start.3 = ((f32[4,4,64,128]{3,2,1,0:T(8,128)}), f32[4,4,64,128]{3,2,1,0:T(8,128)S(1)}, u32[]{:S(2)}, u32[]{:S(2)}) async-start(f32[4,4,64,128]{3,2,1,0:T(8,128)} %bitcast.8), calls=%async_computation.3 | async-start | bytes 1048576 | tf_op jit(solution)/shard_map/all_to_all | solution.py:145
  99.2 0.1 collective-permute-start.2
  99.3 7.2 %all-to-all-done.3 = f32[4,4,64,128]{3,2,1,0:T(8,128)S(1)} async-done(((f32[4,4,64,128]{3,2,1,0:T(8,128)}), f32[4,4,64,128]{3,2,1,0:T(8,128)S(1)}, u32[]{:S(2)}, u32[]{:S(2)}) %all-to-all-start.3) | async-done | bytes 524320 | tf_op jit(solution)/shard_map/all_to_all | solution.py:145
  106.5 0.7 reduce_sum.54
  107.2 3.3 %all-to-all-start.4 = ((f32[4,64,128]{2,1,0:T(8,128)}), f32[4,64,128]{2,1,0:T(8,128)S(1)}, u32[]{:S(2)}, u32[]{:S(2)}) async-start(f32[4,64,128]{2,1,0:T(8,128)} %reduce_sum.54), calls=%async_computation.4 | async-start | bytes 262144 | tf_op jit(solution)/shard_map/all_to_all | solution.py:145
  110.5 0.0 collective-permute-done.2
  110.5 5.9 %all-to-all-done.4 = f32[4,64,128]{2,1,0:T(8,128)S(1)} async-done(((f32[4,64,128]{2,1,0:T(8,128)}), f32[4,64,128]{2,1,0:T(8,128)S(1)}, u32[]{:S(2)}, u32[]{:S(2)}) %all-to-all-start.4) | async-done | bytes 131104 | tf_op jit(solution)/shard_map/all_to_all | solution.py:145
  116.4 1.9 collective-permute-start.3
  118.4 12.7 %collective-permute-done.3 = f32[2,64,128]{2,1,0:T(8,128)S(1)} collective-permute-done((f32[2,64,128]{2,1,0:T(8,128)S(1)}, f32[2,64,128]{2,1,0:T(8,128)S(1)}, u32[]{:S(2)}, u32[]{:S(2)}) %collective-permute-start.3) | collective-permute-done | bytes 65568 | tf_op jit(solution)/shard_map/ppermute | solution.py:154
  131.0 0.1 collective-permute-start.4
  131.1 0.7 broadcast_in_dim.21
  131.8 3.3 %all-to-all-start.6 = ((f32[4,64,128]{2,1,0:T(8,128)}), f32[4,64,128]{2,1,0:T(8,128)S(1)}, u32[]{:S(2)}, u32[]{:S(2)}) async-start(f32[4,64,128]{2,1,0:T(8,128)} %broadcast_in_dim.21), calls=%async_computation.6 | async-start | bytes 262144 | tf_op jit(solution)/shard_map/all_to_all | solution.py:145
  135.1 3.9 %collective-permute-done.4 = f32[64,128]{1,0:T(8,128)S(1)} collective-permute-done((f32[64,128]{1,0:T(8,128)S(1)}, f32[64,128]{1,0:T(8,128)S(1)}, u32[]{:S(2)}, u32[]{:S(2)}) %collective-permute-start.4) | collective-permute-done | bytes 32800 | tf_op jit(solution)/shard_map/ppermute | solution.py:158
  139.0 2.0 all-to-all-done.6
  141.1 12.8 %all_to_all.62 = f32[8,2,64,128]{3,2,1,0:T(8,128)S(1)} all-to-all(f32[8,2,64,128]{3,2,1,0:T(8,128)S(1)} %broadcast_in_dim.23), channel_id=1, replica_groups={{0,16,32,48,64,80,96,112},{128,144,160,176,192,208,224,240},{1,17,33,49..., dimensions={0} | all-to-all | bytes 1048576 | tf_op jit(solution)/shard_map/all_to_all | solution.py:145
  153.9 0.9 broadcast_in_dim.22
  154.7 5.5 %all-to-all-start.7 = ((f32[4,4,64,128]{3,2,1,0:T(8,128)}), f32[4,4,64,128]{3,2,1,0:T(8,128)S(1)}, u32[]{:S(2)}, u32[]{:S(2)}) async-start(f32[4,4,64,128]{3,2,1,0:T(8,128)} %broadcast_in_dim.22), calls=%async_computation.7 | async-start | bytes 1048576 | tf_op jit(solution)/shard_map/all_to_all | solution.py:145
  160.2 7.3 %all-to-all-done.7 = f32[4,4,64,128]{3,2,1,0:T(8,128)S(1)} async-done(((f32[4,4,64,128]{3,2,1,0:T(8,128)}), f32[4,4,64,128]{3,2,1,0:T(8,128)S(1)}, u32[]{:S(2)}, u32[]{:S(2)}) %all-to-all-start.7) | async-done | bytes 524320 | tf_op jit(solution)/shard_map/all_to_all | solution.py:145
  167.5 0.0 copy-start.1
  167.5 3.4 %copy-done.1 = f32[2048,1024]{1,0:T(8,128)S(1)} copy-done((f32[2048,1024]{1,0:T(8,128)S(1)}, f32[2048,1024]{1,0:T(8,128)}, u32[]{:S(2)}) %copy-start.1) | copy-done | bytes 8388632
  170.9 14.7 %shard_map.29 = (f32[16,64,128]{2,1,0:T(8,128)}, f32[16,64,128]{2,1,0:T(8,128)S(1)}) custom-call(s32[3]{0:T(128)S(1)} %pad_add_fusion.where_ref, f32[2048,1024]{1,0:T(8,128)S(1)} %copy-done.1, f32[16,64,128]{2,1,0:T(8,128)S(1)} %bitcast.50, f32[16,64,128]{2,1,0:T(8,128)S(1)} %bitcast.51), custom_call_target="tpu_custom_call" | custom-call | flops 6000000000 | bytes 10000000 | tf_op jit(solution)/shard_map/pallas_call | solution.py:120
  185.6 12.8 %all_to_all.63 = f32[8,2,64,128]{3,2,1,0:T(8,128)S(1)} all-to-all(f32[8,2,64,128]{3,2,1,0:T(8,128)S(1)} %bitcast.58), channel_id=1, replica_groups={{0,16,32,48,64,80,96,112},{128,144,160,176,192,208,224,240},{1,17,33,49..., dimensions={0} | all-to-all | bytes 1048576 | tf_op jit(solution)/shard_map/all_to_all | solution.py:145
  198.4 9.2 %all-to-all-start.9 = ((f32[4,4,64,128]{3,2,1,0:T(8,128)}), f32[4,4,64,128]{3,2,1,0:T(8,128)S(1)}, u32[]{:S(2)}, u32[]{:S(2)}) async-start(f32[4,4,64,128]{3,2,1,0:T(8,128)} %bitcast.22), calls=%async_computation.9 | async-start | bytes 1048576 | tf_op jit(solution)/shard_map/all_to_all | solution.py:145
  207.7 3.2 %collective-permute-start.5 = (f32[64,128]{1,0:T(8,128)S(1)}, f32[64,128]{1,0:T(8,128)S(1)}, u32[]{:S(2)}, u32[]{:S(2)}) collective-permute-start(f32[64,128]{1,0:T(8,128)S(1)} %select_bitcast_fusion), channel_id=1, source_target_pairs={{0,128},{16,144},{32,160},{48,176},{64,192},{80,208},{96,224},{112... | collective-permute-start | bytes 98312 | tf_op jit(solution)/shard_map/ppermute | solution.py:158
  210.9 4.1 %all-to-all-done.9 = f32[4,4,64,128]{3,2,1,0:T(8,128)S(1)} async-done(((f32[4,4,64,128]{3,2,1,0:T(8,128)}), f32[4,4,64,128]{3,2,1,0:T(8,128)S(1)}, u32[]{:S(2)}, u32[]{:S(2)}) %all-to-all-start.9) | async-done | bytes 524320 | tf_op jit(solution)/shard_map/all_to_all | solution.py:145
  215.0 0.7 reduce_sum.57
  215.6 3.3 %all-to-all-start.10 = ((f32[4,64,128]{2,1,0:T(8,128)}), f32[4,64,128]{2,1,0:T(8,128)S(1)}, u32[]{:S(2)}, u32[]{:S(2)}) async-start(f32[4,64,128]{2,1,0:T(8,128)} %reduce_sum.57), calls=%async_computation.10 | async-start | bytes 262144 | tf_op jit(solution)/shard_map/all_to_all | solution.py:145
  219.0 0.0 collective-permute-done.5
  219.0 6.5 %collective-permute-start.6 = (f32[64,128]{1,0:T(8,128)S(1)}, f32[64,128]{1,0:T(8,128)S(1)}, u32[]{:S(2)}, u32[]{:S(2)}) collective-permute-start(f32[64,128]{1,0:T(8,128)S(1)} %bitcast_add_fusion), channel_id=1, source_target_pairs={{0,0},{1,16},{2,32},{3,48},{4,64},{5,80},{6,96},{7,112},{8,128},{9... | collective-permute-start | bytes 98312 | tf_op jit(solution)/shard_map/ppermute | solution.py:154
  225.5 0.0 all-to-all-done.10
  225.5 7.7 %collective-permute-done.6 = f32[64,128]{1,0:T(8,128)S(1)} collective-permute-done((f32[64,128]{1,0:T(8,128)S(1)}, f32[64,128]{1,0:T(8,128)S(1)}, u32[]{:S(2)}, u32[]{:S(2)}) %collective-permute-start.6) | collective-permute-done | bytes 32800 | tf_op jit(solution)/shard_map/ppermute | solution.py:154
  233.2 0.6 add_multiply_fusion
  (20 shorter events, 0.4 us)
Async XLA Ops:
  0.0 14.7 %collective-permute-start = (f32[64,128]{1,0:T(8,128)}, f32[64,128]{1,0:T(8,128)S(1)}, u32[]{:S(2)}, u32[]{:S(2)}) collective-permute-start(f32[64,128]{1,0:T(8,128)} %param.2), channel_id=1, source_target_pairs={{0,0},{1,16},{2,32},{3,48},{4,64},{5,80},{6,96},{7,112},{8,128},{9... | collective-permute-start | bytes 98312 | tf_op jit(solution)/shard_map/ppermute | solution.py:154
  14.7 7.9 %collective-permute-start.1 = (f32[64,128]{1,0:T(8,128)S(1)}, f32[64,128]{1,0:T(8,128)S(1)}, u32[]{:S(2)}, u32[]{:S(2)}) collective-permute-start(f32[64,128]{1,0:T(8,128)S(1)} %collective-permute-done), channel_id=1, source_target_pairs={{0,128},{16,144},{32,160},{48,176},{64,192},{80,208},{96,224},{112... | collective-permute-start | bytes 98312 | tf_op jit(solution)/shard_map/ppermute | solution.py:158
  17.0 11.2 %all-to-all-start = ((f32[4,64,128]{2,1,0:T(8,128)}), f32[4,64,128]{2,1,0:T(8,128)S(1)}, u32[]{:S(2)}, u32[]{:S(2)}) async-start(f32[4,64,128]{2,1,0:T(8,128)} %broadcast_in_dim.18), calls=%async_computation | async-start | bytes 262144 | tf_op jit(solution)/shard_map/all_to_all | solution.py:145
  41.9 17.2 %all-to-all-start.1 = ((f32[4,4,64,128]{3,2,1,0:T(8,128)}), f32[4,4,64,128]{3,2,1,0:T(8,128)S(1)}, u32[]{:S(2)}, u32[]{:S(2)}) async-start(f32[4,4,64,128]{3,2,1,0:T(8,128)} %broadcast_in_dim.19), calls=%async_computation.1 | async-start | bytes 1048576 | tf_op jit(solution)/shard_map/all_to_all | solution.py:145
  59.1 3.4 %copy-start = (f32[2048,1024]{1,0:T(8,128)S(1)}, f32[2048,1024]{1,0:T(8,128)}, u32[]{:S(2)}) copy-start(f32[2048,1024]{1,0:T(8,128)} %values_ref.3) | copy-start | bytes 25165828
  90.0 16.5 %all-to-all-start.3 = ((f32[4,4,64,128]{3,2,1,0:T(8,128)}), f32[4,4,64,128]{3,2,1,0:T(8,128)S(1)}, u32[]{:S(2)}, u32[]{:S(2)}) async-start(f32[4,4,64,128]{3,2,1,0:T(8,128)} %bitcast.8), calls=%async_computation.3 | async-start | bytes 1048576 | tf_op jit(solution)/shard_map/all_to_all | solution.py:145
  99.2 11.3 %collective-permute-start.2 = (f32[64,128]{1,0:T(8,128)S(1)}, f32[64,128]{1,0:T(8,128)S(1)}, u32[]{:S(2)}, u32[]{:S(2)}) collective-permute-start(f32[64,128]{1,0:T(8,128)S(1)} %select_bitcast_fusion.3), channel_id=1, source_target_pairs={{0,128},{16,144},{32,160},{48,176},{64,192},{80,208},{96,224},{112... | collective-permute-start | bytes 98312 | tf_op jit(solution)/shard_map/ppermute | solution.py:158
  107.2 9.2 %all-to-all-start.4 = ((f32[4,64,128]{2,1,0:T(8,128)}), f32[4,64,128]{2,1,0:T(8,128)S(1)}, u32[]{:S(2)}, u32[]{:S(2)}) async-start(f32[4,64,128]{2,1,0:T(8,128)} %reduce_sum.54), calls=%async_computation.4 | async-start | bytes 262144 | tf_op jit(solution)/shard_map/all_to_all | solution.py:145
  116.4 14.6 %collective-permute-start.3 = (f32[2,64,128]{2,1,0:T(8,128)S(1)}, f32[2,64,128]{2,1,0:T(8,128)S(1)}, u32[]{:S(2)}, u32[]{:S(2)}) collective-permute-start(f32[2,64,128]{2,1,0:T(8,128)S(1)} %pad_maximum_fusion.1), channel_id=1, source_target_pairs={{0,0},{1,16},{2,32},{3,48},{4,64},{5,80},{6,96},{7,112},{8,128},{9... | collective-permute-start | bytes 196616 | tf_op jit(solution)/shard_map/ppermute | solution.py:154
  131.0 8.0 %collective-permute-start.4 = (f32[64,128]{1,0:T(8,128)S(1)}, f32[64,128]{1,0:T(8,128)S(1)}, u32[]{:S(2)}, u32[]{:S(2)}) collective-permute-start(f32[64,128]{1,0:T(8,128)S(1)} %get-tuple-element.15), channel_id=1, source_target_pairs={{0,128},{16,144},{32,160},{48,176},{64,192},{80,208},{96,224},{112... | collective-permute-start | bytes 98312 | tf_op jit(solution)/shard_map/ppermute | solution.py:158
  131.8 9.2 %all-to-all-start.6 = ((f32[4,64,128]{2,1,0:T(8,128)}), f32[4,64,128]{2,1,0:T(8,128)S(1)}, u32[]{:S(2)}, u32[]{:S(2)}) async-start(f32[4,64,128]{2,1,0:T(8,128)} %broadcast_in_dim.21), calls=%async_computation.6 | async-start | bytes 262144 | tf_op jit(solution)/shard_map/all_to_all | solution.py:145
  154.7 12.8 %all-to-all-start.7 = ((f32[4,4,64,128]{3,2,1,0:T(8,128)}), f32[4,4,64,128]{3,2,1,0:T(8,128)S(1)}, u32[]{:S(2)}, u32[]{:S(2)}) async-start(f32[4,4,64,128]{3,2,1,0:T(8,128)} %broadcast_in_dim.22), calls=%async_computation.7 | async-start | bytes 1048576 | tf_op jit(solution)/shard_map/all_to_all | solution.py:145
  167.5 3.4 %copy-start.1 = (f32[2048,1024]{1,0:T(8,128)S(1)}, f32[2048,1024]{1,0:T(8,128)}, u32[]{:S(2)}) copy-start(f32[2048,1024]{1,0:T(8,128)} %values_ref.3) | copy-start | bytes 25165828
  198.4 16.5 %all-to-all-start.9 = ((f32[4,4,64,128]{3,2,1,0:T(8,128)}), f32[4,4,64,128]{3,2,1,0:T(8,128)S(1)}, u32[]{:S(2)}, u32[]{:S(2)}) async-start(f32[4,4,64,128]{3,2,1,0:T(8,128)} %bitcast.22), calls=%async_computation.9 | async-start | bytes 1048576 | tf_op jit(solution)/shard_map/all_to_all | solution.py:145
  207.7 11.3 %collective-permute-start.5 = (f32[64,128]{1,0:T(8,128)S(1)}, f32[64,128]{1,0:T(8,128)S(1)}, u32[]{:S(2)}, u32[]{:S(2)}) collective-permute-start(f32[64,128]{1,0:T(8,128)S(1)} %select_bitcast_fusion), channel_id=1, source_target_pairs={{0,128},{16,144},{32,160},{48,176},{64,192},{80,208},{96,224},{112... | collective-permute-start | bytes 98312 | tf_op jit(solution)/shard_map/ppermute | solution.py:158
  215.6 9.9 %all-to-all-start.10 = ((f32[4,64,128]{2,1,0:T(8,128)}), f32[4,64,128]{2,1,0:T(8,128)S(1)}, u32[]{:S(2)}, u32[]{:S(2)}) async-start(f32[4,64,128]{2,1,0:T(8,128)} %reduce_sum.57), calls=%async_computation.10 | async-start | bytes 262144 | tf_op jit(solution)/shard_map/all_to_all | solution.py:145
  219.0 14.2 %collective-permute-start.6 = (f32[64,128]{1,0:T(8,128)S(1)}, f32[64,128]{1,0:T(8,128)S(1)}, u32[]{:S(2)}, u32[]{:S(2)}) collective-permute-start(f32[64,128]{1,0:T(8,128)S(1)} %bitcast_add_fusion), channel_id=1, source_target_pairs={{0,0},{1,16},{2,32},{3,48},{4,64},{5,80},{6,96},{7,112},{8,128},{9... | collective-permute-start | bytes 98312 | tf_op jit(solution)/shard_map/ppermute | solution.py:154

commit v2 on v1

v2 whole, which is shorter than its diff:
```python
import jax
import jax.numpy as jnp
from jax import lax
from jax.experimental import pallas as pl
from jax.experimental.pallas import tpu as pltpu
from jax.sharding import PartitionSpec as P

ITERS = 2
DIMS = 64
PIECE = 128
CHUNK = 256
TALL = 512
WIDE = 512
HALF = 4
BLOCK = 8
STACK = 3 * DIMS + 16
SAMPLES = 32768

Z_GROUPS = [[4 * x + z for z in range(4)] for x in range(4)]
YC_GROUPS = [list(range(8)), list(range(8, 16))]
SHIFTS = (1, 3, 2)


def nn(a, b):
    return lax.dot_general(a, b, (((1,), (0,)), ((), ())), preferred_element_type=jnp.float32)


def tile_kernel(
    where_ref, values_ref, r0, r1, r2, r3, cols_ref, o0, o1, o2, o3, cols_out,
    left, right, stack, table, norm_i, norm_j, acc, acc_lead,
):
    step = pl.program_id(0)
    lead_base, trail_base, diagonal = where_ref[0], where_ref[1], where_ref[2]
    x_pos, z_pos = where_ref[3], where_ref[4]

    def at(n, length=CHUNK):
        return pl.ds(pl.multiple_of(n * CHUNK, CHUNK), length)

    def chunks(row_refs, col_ref, send):
        for ref, shift in zip(row_refs, (0, *SHIFTS)):
            group = lax.rem(x_pos + (shift if send else 4 - shift), 4)
            for m in range(2):
                yield 2 * group + m, ref.at[2 * m], ref.at[2 * m + 1]
        for s in range(2):
            half = z_pos if s == 0 else 1 - z_pos
            for m in range(4):
                yield BLOCK + 4 * half + m, col_ref.at[2 * m, s], col_ref.at[2 * m + 1, s]

    inputs = lambda: chunks((r0, r1, r2, r3), cols_ref, False)

    @pl.when(step == 0)
    def _():
        acc[...] = jnp.zeros_like(acc)
        acc_lead[...] = jnp.zeros_like(acc_lead)
        ones = jnp.ones((16, CHUNK), jnp.bfloat16)
        for n, a, b in inputs():
            x = jnp.concatenate([a[...], b[...]], axis=1)
            hi = x.astype(jnp.bfloat16)
            hi32 = hi.astype(jnp.float32)
            rest = x - hi32
            mid = rest.astype(jnp.bfloat16)
            mid32 = mid.astype(jnp.float32)
            lo = (rest - mid32).astype(jnp.bfloat16)
            stack[:, at(n)] = jnp.concatenate([hi, mid, lo, ones], axis=0)
            right[:, at(n)] = -2.0 * jnp.concatenate([hi, mid, mid, hi], axis=0)
            main = jnp.concatenate([hi32, mid32], axis=0).T.astype(jnp.bfloat16)
            tail = jnp.concatenate([lo.astype(jnp.float32), jnp.ones_like(x)], axis=0).T.astype(jnp.bfloat16)
            left[at(n), :] = jnp.concatenate([main, main], axis=1)
            table[at(n), :] = jnp.concatenate([main, tail], axis=1)
            near = hi32 + mid32
            norms = jnp.sum(near * near, axis=0, keepdims=True)
            norm_j[:, at(n)] = jnp.broadcast_to(norms + 1.0, (8, CHUNK))
            norm_i[at(n), :] = jnp.broadcast_to(norms, (PIECE, CHUNK)).T

    def ratios_of(values, lead, trail):
        inner = nn(left[at(lead, values.shape[0]), :], right[:, at(trail, values.shape[1])])
        ni = jnp.concatenate([norm_i[at(lead, values.shape[0]), :]] * (values.shape[1] // PIECE), axis=1)
        squared = inner + (ni + norm_j[0:1, at(trail, values.shape[1])])
        return values * lax.rsqrt(squared)

    def products(ratios, lead, trail):
        tall, wide = ratios.shape
        hi = ratios.astype(jnp.bfloat16)
        lo = (ratios - hi.astype(jnp.float32)).astype(jnp.bfloat16)
        above, beside = stack[:, at(lead, tall)], table[at(trail, wide), :]
        acc[:, at(trail, wide)] += nn(above, hi) + nn(above, lo)
        acc_lead[at(lead - lead_base, tall), :] += nn(hi, beside) + nn(lo, beside)

    special = jnp.logical_and(diagonal == 1, step < 2)

    @pl.when(jnp.logical_not(special))
    def _():
        lead = lead_base + 2 * step
        for j in range(0, 1024, WIDE):
            trail = trail_base + j // CHUNK
            products(ratios_of(values_ref[:, j : j + WIDE], lead, trail), lead, trail)

    @pl.when(special)
    def _():
        row_iota = lax.broadcasted_iota(jnp.int32, (CHUNK, CHUNK), 0)
        col_iota = lax.broadcasted_iota(jnp.int32, (CHUNK, CHUNK), 1)
        for i in range(2):
            here = 2 * step + i
            for j in range(HALF):
                values = values_ref[i * CHUNK : (i + 1) * CHUNK, j * CHUNK : (j + 1) * CHUNK]

                @pl.when(here != j)
                def _():
                    shift = jnp.where(here > j, HALF, 0)
                    products(ratios_of(values, here + shift, j + shift), here + shift, j + shift)

                @pl.when(here == j)
                def _():
                    for shift, keep in ((0, col_iota > row_iota), (HALF, col_iota < row_iota)):
                        ratios = jnp.where(keep, ratios_of(values, j + shift, j + shift), 0.0)
                        products(ratios, j + shift, j + shift)

    @pl.when(step == pl.num_programs(0) - 1)
    def _():
        for n in range(BLOCK):
            acc[:, at(lead_base + n)] += acc_lead[n * CHUNK : (n + 1) * CHUNK, :].T[:STACK]

        def terms_of(n, a, b):
            x = jnp.concatenate([a[...], b[...]], axis=1)
            part = acc[:, at(n)]
            pulled = part[0:DIMS] + part[DIMS : 2 * DIMS] + part[2 * DIMS : 3 * DIMS]
            return x * part[3 * DIMS : 3 * DIMS + 1] - pulled

        by_send = ((r0, o0), (r2, o1), (r1, o2), (r3, o3))
        sources = list(chunks([a for a, _ in by_send], cols_ref, True))
        targets = list(chunks([b for _, b in by_send], cols_out, True))
        for (n, a, b), (_, c, d) in zip(sources, targets):
            terms = terms_of(n, a, b)
            c[...] = terms[:, :PIECE]
            d[...] = terms[:, PIECE:]


def tile_terms(where, values, groups, cols):
    row_shape = jax.ShapeDtypeStruct(groups[0].shape, jnp.float32)
    col_shape = jax.ShapeDtypeStruct(cols.shape, jnp.float32)
    row_spec = pl.BlockSpec(row_shape.shape, lambda i, w: (0, 0, 0))
    col_spec = pl.BlockSpec(col_shape.shape, lambda i, w: (0, 0, 0, 0))
    total = 2 * BLOCK * CHUNK
    return pl.pallas_call(
        tile_kernel,
        out_shape=(row_shape,) * 4 + (col_shape,),
        grid_spec=pltpu.PrefetchScalarGridSpec(
            num_scalar_prefetch=1,
            grid=(values.shape[0] // TALL,),
            in_specs=[pl.BlockSpec((TALL, values.shape[1]), lambda i, w: (i, 0))] + [row_spec] * 4 + [col_spec],
            out_specs=(row_spec,) * 4 + (col_spec,),
            scratch_shapes=[
                pltpu.VMEM((total, CHUNK), jnp.bfloat16),
                pltpu.VMEM((CHUNK, total), jnp.bfloat16),
                pltpu.VMEM((STACK, total), jnp.bfloat16),
                pltpu.VMEM((total, CHUNK), jnp.bfloat16),
                pltpu.VMEM((total, PIECE), jnp.float32),
                pltpu.VMEM((8, total), jnp.float32),
                pltpu.VMEM((STACK, total), jnp.float32),
                pltpu.VMEM((total // 2, CHUNK), jnp.float32),
            ],
        ),
        compiler_params=pltpu.CompilerParams(
            dimension_semantics=("arbitrary",), vmem_limit_bytes=56 * 1024 * 1024
        ),
        cost_estimate=pl.CostEstimate(flops=6_000_000_000, transcendentals=2_097_152, bytes_accessed=10_000_000),
    )(where, values, *groups, cols)


def exchange(x, axis, groups):
    return lax.all_to_all(x, axis, split_axis=0, concat_axis=0, tiled=True, axis_index_groups=groups)


def spread(x, axis, groups):
    return exchange(jnp.broadcast_to(x, (len(groups[0]), *x.shape)), axis, groups)


def transposed(x):
    pairs = [(a * 16 + b, b * 16 + a) for a in range(16) for b in range(16)]
    return lax.ppermute(x, ("row", "col"), pairs)


def across(x):
    return lax.ppermute(x, "row", [(a, (a + 8) % 16) for a in range(16)])


def along(x, shift):
    return lax.ppermute(x, "col", [(a, (a + 4 * shift) % 16) for a in range(16)])


def gathered(own, turned):
    line = spread(own, "col", Z_GROUPS)
    other = across(turned)
    cols = spread(jnp.stack([turned, other]), "row", YC_GROUPS)
    return (line, *(along(line, s) for s in SHIFTS)), cols


def reduced(groups, cols):
    kept, sent = exchange(cols, "row", YC_GROUPS).sum(axis=0)
    line = groups[0]
    for part, s in zip(groups[1:], SHIFTS):
        line = line + along(part, s)
    came = across(sent)
    row_sum = exchange(line, "col", Z_GROUPS).sum(axis=0)
    return row_sum, kept + came


def local(coords, dissimilarity):
    row, col = lax.axis_index("row"), lax.axis_index("col")
    lead_base = jnp.where(row > col, BLOCK, 0)
    trail_base = jnp.where(row < col, BLOCK, jnp.where(row > col, HALF, 0))
    diagonal = (row == col).astype(jnp.int32)
    where = jnp.stack([lead_base, trail_base, diagonal, col // 4, row // 8]).astype(jnp.int32)
    own, turned = coords, transposed(coords)
    scale = 1.0 / SAMPLES
    for iteration in range(ITERS):
        groups, cols = gathered(own, turned)
        *groups, cols = tile_terms(where, dissimilarity, groups, cols)
        row_sum, col_sum = reduced(groups, cols)
        if iteration + 1 < ITERS:
            came = transposed(jnp.stack([row_sum, col_sum]))
            own = (row_sum + came[1]) * scale
            turned = (col_sum + came[0]) * scale
        else:
            own = (row_sum + transposed(col_sum)) * scale
    return own


def solution(mesh):
    in_specs = (P(None, ("row", "col")), P("row", "col"))
    out_specs = P(None, ("row", "col"))
    return jax.shard_map(local, mesh=mesh, in_specs=in_specs, out_specs=out_specs, check_vma=False)
```

time: 235 us -> 195 us (0.83)
  blocking collectives: 51.2 us -> 0 us
  starting transfers between devices: 73.3 us -> 94.6 us
  waiting for transfers between devices: 66.8 us -> 62.2 us
  local copies, waits for them, and re-layouts: 10.8 us -> 6.75 us
  Pallas kernels: 29.4 us -> 26 us
    all_to_all x4 -> x0, blocking collectives: 51.2 us -> none  [exchange(): lax.all_to_all(x, axis, split_axis=0, concat_axis=0, tiled=True, axis_ind...]
    all_to_all x8, waiting for transfers between devices: 39.2 us -> 5.29 us  [exchange(): lax.all_to_all(x, axis, split_axis=0, concat_axis=0, tiled=True, axis_ind...]
    ppermute x0 -> x12, starting transfers between devices: none -> 25.5 us  [along(): lax.ppermute(x, 'col', [(a, (a + 4 * shift) % 16) for a in range(16)])]
    ppermute x0 -> x12, waiting for transfers between devices: none -> 19 us  [along(): lax.ppermute(x, 'col', [(a, (a + 4 * shift) % 16) for a in range(16)])]
    all_to_all x8, starting transfers between devices: 48.9 us -> 32.6 us  [exchange(): lax.all_to_all(x, axis, split_axis=0, concat_axis=0, tiled=True, axis_ind...]
    ppermute x4, waiting for transfers between devices: 4.2 us -> 17.2 us  [across(): return lax.ppermute(x, 'row', [(a, (a + 8) % 16) for a in range(16)])]
    ppermute x4, starting transfers between devices: 4.3 us -> 13.5 us  [across(): return lax.ppermute(x, 'row', [(a, (a + 8) % 16) for a in range(16)])]
    unnamed x4 -> x20, local copies, waits for them, and re-layouts: 6.76 us -> 2.29 us
  transfers between devices with their start and end apart: 15 -> 27, of which waited for: 12 -> 17; matrix products, arithmetic and copies ran while one was open for 2% -> 2% of each run, Pallas kernels for 0% -> 0%
where the time goes in v2:
time: 195 us; the launch traced here: 194 us
  starting transfers between devices  94.6 us (49%)
  waiting for transfers between devices  62.2 us (32%)
  Pallas kernels  26 us (13%)
  local copies, waits for them, and re-layouts  6.75 us (3%)
  other arithmetic  3.91 us (2%)
    all_to_all x8, starting transfers between devices, exchange(): lax.all_to_all(x, axis, split_axis=0, concat_axis=0, tiled=True, axis_ind...  32.6 us
    pallas_call x2, Pallas kernels, tile_terms(): pl.pallas_call(tile_kernel, out_shape=(row_shape,) * 4 + (col_shape,), gr...  26 us
    ppermute x12, starting transfers between devices, along(): lax.ppermute(x, 'col', [(a, (a + 4 * shift) % 16) for a in range(16)])  25.5 us
    ppermute x3, starting transfers between devices, transposed(): return lax.ppermute(x, ('row', 'col'), pairs)  23.1 us
    ppermute x3, waiting for transfers between devices, transposed(): return lax.ppermute(x, ('row', 'col'), pairs)  20.6 us
    ppermute x12, waiting for transfers between devices, along(): lax.ppermute(x, 'col', [(a, (a + 4 * shift) % 16) for a in range(16)])  19 us
    ppermute x4, waiting for transfers between devices, across(): return lax.ppermute(x, 'row', [(a, (a + 8) % 16) for a in range(16)])  17.2 us
    ppermute x4, starting transfers between devices, across(): return lax.ppermute(x, 'row', [(a, (a + 8) % 16) for a in range(16)])  13.5 us
  transfers between devices with their start and end apart: 27, of which 17 were waited for; matrix products, arithmetic and copies ran while one was open for 2% of the time, Pallas kernels for 0%

profile of v2, /device:TPU:6, one launch (start us, length us, event | category | flops | bytes accessed | tf_op | source)
XLA Modules:
  0.0 193.6 jit_solution(7825116534792510860)
XLA Ops:
  0.0 1.4 broadcast_in_dim.12
  1.4 5.9 %all-to-all-start = ((f32[4,64,128]{2,1,0:T(8,128)}), f32[4,64,128]{2,1,0:T(8,128)S(1)}, u32[]{:S(2)}, u32[]{:S(2)}) async-start(f32[4,64,128]{2,1,0:T(8,128)} %broadcast_in_dim.12), calls=%async_computation | async-start | bytes 262144 | tf_op jit(solution)/shard_map/all_to_all | solution.py:171
  7.3 9.1 %collective-permute-start.3 = (f32[64,128]{1,0:T(8,128)}, f32[64,128]{1,0:T(8,128)S(1)}, u32[]{:S(2)}, u32[]{:S(2)}) collective-permute-start(f32[64,128]{1,0:T(8,128)} %param.2), channel_id=1, source_target_pairs={{0,0},{1,16},{2,32},{3,48},{4,64},{5,80},{6,96},{7,112},{8,128},{9... | collective-permute-start | bytes 98312 | tf_op jit(solution)/shard_map/ppermute | solution.py:180
  16.4 5.3 %collective-permute-done.3 = f32[64,128]{1,0:T(8,128)S(1)} collective-permute-done((f32[64,128]{1,0:T(8,128)}, f32[64,128]{1,0:T(8,128)S(1)}, u32[]{:S(2)}, u32[]{:S(2)}) %collective-permute-start.3) | collective-permute-done | bytes 32800 | tf_op jit(solution)/shard_map/ppermute | solution.py:180
  21.7 8.2 %collective-permute-done.4 = f32[64,128]{1,0:T(8,128)S(1)} collective-permute-done((f32[64,128]{1,0:T(8,128)S(1)}, f32[64,128]{1,0:T(8,128)S(1)}, u32[]{:S(2)}, u32[]{:S(2)}) %collective-permute-start.4) | collective-permute-done | bytes 32800 | tf_op jit(solution)/shard_map/ppermute | solution.py:184
  29.9 0.0 all-to-all-done.r0
  29.9 0.8 broadcast_in_dim.13
  30.8 3.5 %all-to-all-start.1 = ((f32[8,2,64,128]{3,2,1,0:T(8,128)}), f32[8,2,64,128]{3,2,1,0:T(8,128)S(1)}, u32[]{:S(2)}, u32[]{:S(2)}) async-start(f32[8,2,64,128]{3,2,1,0:T(8,128)} %broadcast_in_dim.13), calls=%async_computation.1 | async-start | bytes 1048576 | tf_op jit(solution)/shard_map/all_to_all | solution.py:171
  34.3 0.1 collective-permute-start.2
  34.4 0.6 collective-permute-start.1
  35.0 2.7 %collective-permute-start = (f32[4,64,128]{2,1,0:T(8,128)S(1)}, f32[4,64,128]{2,1,0:T(8,128)S(1)}, u32[]{:S(2)}, u32[]{:S(2)}) collective-permute-start(f32[4,64,128]{2,1,0:T(8,128)S(1)} %all-to-all-done.r0), channel_id=1, source_target_pairs={{0,4},{1,5},{2,6},{3,7},{4,8},{5,9},{6,10},{7,11},{8,12},{9,13},{1... | collective-permute-start | bytes 393224 | tf_op jit(solution)/shard_map/ppermute | solution.py:188
  37.7 0.7 stack.54.where_ref
  38.4 3.9 %collective-permute-done.2.r3 = f32[4,64,128]{2,1,0:T(8,128)S(1)} collective-permute-done((f32[4,64,128]{2,1,0:T(8,128)S(1)}, f32[4,64,128]{2,1,0:T(8,128)S(1)}, u32[]{:S(2)}, u32[]{:S(2)}) %collective-permute-start.2) | collective-permute-done | bytes 131104 | tf_op jit(solution)/shard_map/ppermute | solution.py:188
  42.2 2.0 %collective-permute-done.1.r2 = f32[4,64,128]{2,1,0:T(8,128)S(1)} collective-permute-done((f32[4,64,128]{2,1,0:T(8,128)S(1)}, f32[4,64,128]{2,1,0:T(8,128)S(1)}, u32[]{:S(2)}, u32[]{:S(2)}) %collective-permute-start.1) | collective-permute-done | bytes 131104 | tf_op jit(solution)/shard_map/ppermute | solution.py:188
  44.2 0.3 all-to-all-done.1.cols_ref
  44.6 0.4 copy-done.5
  44.9 0.0 copy-done.6
  44.9 0.8 copy-done
  45.8 13.0 %shard_map.28 = (f32[4,64,128]{2,1,0:T(8,128)}, f32[4,64,128]{2,1,0:T(8,128)}, f32[4,64,128]{2,1,0:T(8,128)}, f32[4,64,128]{2,1,0:T(8,128)}, f32[8,2,64,128]{3,2,1,0:T(8,128)}) custom-call(s32[5]{0:T(128)} %stack.54.where_ref, f32[2048,1024]{1,0:T(8,128)} %values_ref.3, f32[4,64,128]{2,1,0:T(8,128)} %copy-done.2, f32[4,64,128]{2,1,0:T(8,128)} %copy-done.6, ...), custom_call_target="tpu_custom_call" | custom-call | flops 6000000000 | bytes 10000000 | tf_op jit(solution)/shard_map/pallas_call | solution.py:144
  58.8 4.4 %all-to-all-start.3 = ((f32[8,2,64,128]{3,2,1,0:T(8,128)}), f32[8,2,64,128]{3,2,1,0:T(8,128)S(1)}, u32[]{:S(2)}, u32[]{:S(2)}) async-start(f32[8,2,64,128]{3,2,1,0:T(8,128)} %get-tuple-element.19), calls=%async_computation.3 | async-start | bytes 1048576 | tf_op jit(solution)/shard_map/all_to_all | solution.py:171
  63.2 6.4 %collective-permute-start.5 = (f32[4,64,128]{2,1,0:T(8,128)}, f32[4,64,128]{2,1,0:T(8,128)S(1)}, u32[]{:S(2)}, u32[]{:S(2)}) collective-permute-start(f32[4,64,128]{2,1,0:T(8,128)} %get-tuple-element.16), channel_id=1, source_target_pairs={{0,4},{1,5},{2,6},{3,7},{4,8},{5,9},{6,10},{7,11},{8,12},{9,13},{1... | collective-permute-start | bytes 393224 | tf_op jit(solution)/shard_map/ppermute | solution.py:188
  69.6 0.0 collective-permute-start.6
  69.6 3.3 %collective-permute-start.7 = (f32[4,64,128]{2,1,0:T(8,128)}, f32[4,64,128]{2,1,0:T(8,128)S(1)}, u32[]{:S(2)}, u32[]{:S(2)}) collective-permute-start(f32[4,64,128]{2,1,0:T(8,128)} %get-tuple-element.18), channel_id=1, source_target_pairs={{0,8},{1,9},{2,10},{3,11},{4,12},{5,13},{6,14},{7,15},{8,0},{9,1},... | collective-permute-start | bytes 393224 | tf_op jit(solution)/shard_map/ppermute | solution.py:188
  73.0 0.0 collective-permute-done.5
  73.0 3.5 %collective-permute-done.6 = f32[4,64,128]{2,1,0:T(8,128)S(1)} collective-permute-done((f32[4,64,128]{2,1,0:T(8,128)}, f32[4,64,128]{2,1,0:T(8,128)S(1)}, u32[]{:S(2)}, u32[]{:S(2)}) %collective-permute-start.6) | collective-permute-done | bytes 131104 | tf_op jit(solution)/shard_map/ppermute | solution.py:188
  76.5 3.1 %collective-permute-done.7 = f32[4,64,128]{2,1,0:T(8,128)S(1)} collective-permute-done((f32[4,64,128]{2,1,0:T(8,128)}, f32[4,64,128]{2,1,0:T(8,128)S(1)}, u32[]{:S(2)}, u32[]{:S(2)}) %collective-permute-start.7) | collective-permute-done | bytes 131104 | tf_op jit(solution)/shard_map/ppermute | solution.py:188
  79.6 1.6 add_add_fusion.1
  81.2 0.0 all-to-all-done.3
  81.2 3.5 %all-to-all-start.2 = ((f32[4,64,128]{2,1,0:T(8,128)}), f32[4,64,128]{2,1,0:T(8,128)S(1)}, u32[]{:S(2)}, u32[]{:S(2)}) async-start(f32[4,64,128]{2,1,0:T(8,128)} %add_add_fusion.1), calls=%async_computation.2 | async-start | bytes 262144 | tf_op jit(solution)/shard_map/all_to_all | solution.py:171
  84.7 3.6 %collective-permute-start.8 = (f32[64,128]{1,0:T(8,128)S(1)}, f32[64,128]{1,0:T(8,128)S(1)}, u32[]{:S(2)}, u32[]{:S(2)}) collective-permute-start(f32[64,128]{1,0:T(8,128)S(1)} %slice_bitcast_fusion.4), channel_id=1, source_target_pairs={{0,128},{16,144},{32,160},{48,176},{64,192},{80,208},{96,224},{112... | collective-permute-start | bytes 98312 | tf_op jit(solution)/shard_map/ppermute | solution.py:184
  88.3 2.3 %all-to-all-done.2 = f32[4,64,128]{2,1,0:T(8,128)S(1)} async-done(((f32[4,64,128]{2,1,0:T(8,128)}), f32[4,64,128]{2,1,0:T(8,128)S(1)}, u32[]{:S(2)}, u32[]{:S(2)}) %all-to-all-start.2) | async-done | bytes 131104 | tf_op jit(solution)/shard_map/all_to_all | solution.py:171
  90.7 2.0 %collective-permute-done.8 = f32[64,128]{1,0:T(8,128)S(1)} collective-permute-done((f32[64,128]{1,0:T(8,128)S(1)}, f32[64,128]{1,0:T(8,128)S(1)}, u32[]{:S(2)}, u32[]{:S(2)}) %collective-permute-start.8) | collective-permute-done | bytes 32800 | tf_op jit(solution)/shard_map/ppermute | solution.py:184
  92.7 8.9 %collective-permute-start.9 = (f32[2,64,128]{2,1,0:T(8,128)S(1)}, f32[2,64,128]{2,1,0:T(8,128)S(1)}, u32[]{:S(2)}, u32[]{:S(2)}) collective-permute-start(f32[2,64,128]{2,1,0:T(8,128)S(1)} %pad_maximum_fusion.1), channel_id=1, source_target_pairs={{0,0},{1,16},{2,32},{3,48},{4,64},{5,80},{6,96},{7,112},{8,128},{9... | collective-permute-start | bytes 196616 | tf_op jit(solution)/shard_map/ppermute | solution.py:180
  101.6 7.0 %collective-permute-done.9 = f32[2,64,128]{2,1,0:T(8,128)S(1)} collective-permute-done((f32[2,64,128]{2,1,0:T(8,128)S(1)}, f32[2,64,128]{2,1,0:T(8,128)S(1)}, u32[]{:S(2)}, u32[]{:S(2)}) %collective-permute-start.9) | collective-permute-done | bytes 65568 | tf_op jit(solution)/shard_map/ppermute | solution.py:180
  108.6 0.7 broadcast_in_dim.14
  109.3 3.3 %all-to-all-start.4 = ((f32[4,64,128]{2,1,0:T(8,128)}), f32[4,64,128]{2,1,0:T(8,128)S(1)}, u32[]{:S(2)}, u32[]{:S(2)}) async-start(f32[4,64,128]{2,1,0:T(8,128)} %broadcast_in_dim.14), calls=%async_computation.4 | async-start | bytes 262144 | tf_op jit(solution)/shard_map/all_to_all | solution.py:171
  112.6 0.8 collective-permute-start.13
  113.4 7.1 %collective-permute-done.13 = f32[64,128]{1,0:T(8,128)S(1)} collective-permute-done((f32[64,128]{1,0:T(8,128)S(1)}, f32[64,128]{1,0:T(8,128)S(1)}, u32[]{:S(2)}, u32[]{:S(2)}) %collective-permute-start.13) | collective-permute-done | bytes 32800 | tf_op jit(solution)/shard_map/ppermute | solution.py:184
  120.5 0.8 broadcast_in_dim.15
  121.4 3.6 %all-to-all-start.5 = ((f32[8,2,64,128]{3,2,1,0:T(8,128)}), f32[8,2,64,128]{3,2,1,0:T(8,128)S(1)}, u32[]{:S(2)}, u32[]{:S(2)}) async-start(f32[8,2,64,128]{3,2,1,0:T(8,128)} %broadcast_in_dim.15), calls=%async_computation.5 | async-start | bytes 1048576 | tf_op jit(solution)/shard_map/all_to_all | solution.py:171
  125.0 0.0 collective-permute-start.12
  125.0 1.3 collective-permute-start.11
  126.3 2.1 %collective-permute-start.10 = (f32[4,64,128]{2,1,0:T(8,128)S(1)}, f32[4,64,128]{2,1,0:T(8,128)S(1)}, u32[]{:S(2)}, u32[]{:S(2)}) collective-permute-start(f32[4,64,128]{2,1,0:T(8,128)S(1)} %all-to-all-done.4.r0), channel_id=1, source_target_pairs={{0,4},{1,5},{2,6},{3,7},{4,8},{5,9},{6,10},{7,11},{8,12},{9,13},{1... | collective-permute-start | bytes 393224 | tf_op jit(solution)/shard_map/ppermute | solution.py:188
  128.3 4.5 %collective-permute-done.12.r3 = f32[4,64,128]{2,1,0:T(8,128)S(1)} collective-permute-done((f32[4,64,128]{2,1,0:T(8,128)S(1)}, f32[4,64,128]{2,1,0:T(8,128)S(1)}, u32[]{:S(2)}, u32[]{:S(2)}) %collective-permute-start.12) | collective-permute-done | bytes 131104 | tf_op jit(solution)/shard_map/ppermute | solution.py:188
  132.9 2.0 %collective-permute-done.11.r2 = f32[4,64,128]{2,1,0:T(8,128)S(1)} collective-permute-done((f32[4,64,128]{2,1,0:T(8,128)S(1)}, f32[4,64,128]{2,1,0:T(8,128)S(1)}, u32[]{:S(2)}, u32[]{:S(2)}) %collective-permute-start.11) | collective-permute-done | bytes 131104 | tf_op jit(solution)/shard_map/ppermute | solution.py:188
  134.9 0.4 all-to-all-done.5.cols_ref
  135.3 0.2 copy-done.8
  135.6 0.0 copy-done.9
  135.6 0.8 copy-done.1
  136.4 13.0 %shard_map.29 = (f32[4,64,128]{2,1,0:T(8,128)}, f32[4,64,128]{2,1,0:T(8,128)}, f32[4,64,128]{2,1,0:T(8,128)}, f32[4,64,128]{2,1,0:T(8,128)}, f32[8,2,64,128]{3,2,1,0:T(8,128)}) custom-call(s32[5]{0:T(128)} %stack.54.where_ref, f32[2048,1024]{1,0:T(8,128)} %values_ref.3, f32[4,64,128]{2,1,0:T(8,128)} %copy-done.3, f32[4,64,128]{2,1,0:T(8,128)} %copy-done.9, ...), custom_call_target="tpu_custom_call" | custom-call | flops 6000000000 | bytes 10000000 | tf_op jit(solution)/shard_map/pallas_call | solution.py:144
  149.4 4.4 %all-to-all-start.7 = ((f32[8,2,64,128]{3,2,1,0:T(8,128)}), f32[8,2,64,128]{3,2,1,0:T(8,128)S(1)}, u32[]{:S(2)}, u32[]{:S(2)}) async-start(f32[8,2,64,128]{3,2,1,0:T(8,128)} %get-tuple-element.24), calls=%async_computation.7 | async-start | bytes 1048576 | tf_op jit(solution)/shard_map/all_to_all | solution.py:171
  153.8 6.6 %collective-permute-start.14 = (f32[4,64,128]{2,1,0:T(8,128)}, f32[4,64,128]{2,1,0:T(8,128)S(1)}, u32[]{:S(2)}, u32[]{:S(2)}) collective-permute-start(f32[4,64,128]{2,1,0:T(8,128)} %get-tuple-element.21), channel_id=1, source_target_pairs={{0,4},{1,5},{2,6},{3,7},{4,8},{5,9},{6,10},{7,11},{8,12},{9,13},{1... | collective-permute-start | bytes 393224 | tf_op jit(solution)/shard_map/ppermute | solution.py:188
  160.5 0.0 collective-permute-start.15
  160.5 2.3 %collective-permute-start.16 = (f32[4,64,128]{2,1,0:T(8,128)}, f32[4,64,128]{2,1,0:T(8,128)S(1)}, u32[]{:S(2)}, u32[]{:S(2)}) collective-permute-start(f32[4,64,128]{2,1,0:T(8,128)} %get-tuple-element.23), channel_id=1, source_target_pairs={{0,8},{1,9},{2,10},{3,11},{4,12},{5,13},{6,14},{7,15},{8,0},{9,1},... | collective-permute-start | bytes 393224 | tf_op jit(solution)/shard_map/ppermute | solution.py:188
  162.8 1.4 all-to-all-done.7
  164.2 9.0 %collective-permute-start.17 = (f32[64,128]{1,0:T(8,128)S(1)}, f32[64,128]{1,0:T(8,128)S(1)}, u32[]{:S(2)}, u32[]{:S(2)}) collective-permute-start(f32[64,128]{1,0:T(8,128)S(1)} %slice_bitcast_fusion), channel_id=1, source_target_pairs={{0,128},{16,144},{32,160},{48,176},{64,192},{80,208},{96,224},{112... | collective-permute-start | bytes 98312 | tf_op jit(solution)/shard_map/ppermute | solution.py:184
  173.3 0.0 collective-permute-done.14
  173.3 0.0 collective-permute-done.15
  173.3 1.6 add_add_fusion
  174.9 3.9 %all-to-all-start.6 = ((f32[4,64,128]{2,1,0:T(8,128)}), f32[4,64,128]{2,1,0:T(8,128)S(1)}, u32[]{:S(2)}, u32[]{:S(2)}) async-start(f32[4,64,128]{2,1,0:T(8,128)} %add_add_fusion), calls=%async_computation.6 | async-start | bytes 262144 | tf_op jit(solution)/shard_map/all_to_all | solution.py:171
  178.8 5.1 %collective-permute-start.18 = (f32[64,128]{1,0:T(8,128)S(1)}, f32[64,128]{1,0:T(8,128)S(1)}, u32[]{:S(2)}, u32[]{:S(2)}) collective-permute-start(f32[64,128]{1,0:T(8,128)S(1)} %fusion), channel_id=1, source_target_pairs={{0,0},{1,16},{2,32},{3,48},{4,64},{5,80},{6,96},{7,112},{8,128},{9... | collective-permute-start | bytes 98312 | tf_op jit(solution)/shard_map/ppermute | solution.py:180
  183.8 0.8 all-to-all-done.6
  184.7 8.3 %collective-permute-done.18 = f32[64,128]{1,0:T(8,128)S(1)} collective-permute-done((f32[64,128]{1,0:T(8,128)S(1)}, f32[64,128]{1,0:T(8,128)S(1)}, u32[]{:S(2)}, u32[]{:S(2)}) %collective-permute-start.18) | collective-permute-done | bytes 32800 | tf_op jit(solution)/shard_map/ppermute | solution.py:180
  193.0 0.6 add_multiply_fusion
  (32 shorter events, 0.2 us)
Async XLA Ops:
  1.4 28.5 %all-to-all-start = ((f32[4,64,128]{2,1,0:T(8,128)}), f32[4,64,128]{2,1,0:T(8,128)S(1)}, u32[]{:S(2)}, u32[]{:S(2)}) async-start(f32[4,64,128]{2,1,0:T(8,128)} %broadcast_in_dim.12), calls=%async_computation | async-start | bytes 262144 | tf_op jit(solution)/shard_map/all_to_all | solution.py:171
  7.3 14.4 %collective-permute-start.3 = (f32[64,128]{1,0:T(8,128)}, f32[64,128]{1,0:T(8,128)S(1)}, u32[]{:S(2)}, u32[]{:S(2)}) collective-permute-start(f32[64,128]{1,0:T(8,128)} %param.2), channel_id=1, source_target_pairs={{0,0},{1,16},{2,32},{3,48},{4,64},{5,80},{6,96},{7,112},{8,128},{9... | collective-permute-start | bytes 98312 | tf_op jit(solution)/shard_map/ppermute | solution.py:180
  21.7 8.2 %collective-permute-start.4 = (f32[64,128]{1,0:T(8,128)S(1)}, f32[64,128]{1,0:T(8,128)S(1)}, u32[]{:S(2)}, u32[]{:S(2)}) collective-permute-start(f32[64,128]{1,0:T(8,128)S(1)} %collective-permute-done.3), channel_id=1, source_target_pairs={{0,128},{16,144},{32,160},{48,176},{64,192},{80,208},{96,224},{112... | collective-permute-start | bytes 98312 | tf_op jit(solution)/shard_map/ppermute | solution.py:184
  29.9 14.6 %copy-start.2 = (f32[4,64,128]{2,1,0:T(8,128)}, f32[4,64,128]{2,1,0:T(8,128)S(1)}, u32[]{:S(2)}) copy-start(f32[4,64,128]{2,1,0:T(8,128)S(1)} %all-to-all-done.r0) | copy-start | bytes 393220
  30.8 13.8 %all-to-all-start.1 = ((f32[8,2,64,128]{3,2,1,0:T(8,128)}), f32[8,2,64,128]{3,2,1,0:T(8,128)S(1)}, u32[]{:S(2)}, u32[]{:S(2)}) async-start(f32[8,2,64,128]{3,2,1,0:T(8,128)} %broadcast_in_dim.13), calls=%async_computation.1 | async-start | bytes 1048576 | tf_op jit(solution)/shard_map/all_to_all | solution.py:171
  34.3 8.0 %collective-permute-start.2 = (f32[4,64,128]{2,1,0:T(8,128)S(1)}, f32[4,64,128]{2,1,0:T(8,128)S(1)}, u32[]{:S(2)}, u32[]{:S(2)}) collective-permute-start(f32[4,64,128]{2,1,0:T(8,128)S(1)} %all-to-all-done.r0), channel_id=1, source_target_pairs={{0,8},{1,9},{2,10},{3,11},{4,12},{5,13},{6,14},{7,15},{8,0},{9,1},... | collective-permute-start | bytes 393224 | tf_op jit(solution)/shard_map/ppermute | solution.py:188
  34.4 9.9 %collective-permute-start.1 = (f32[4,64,128]{2,1,0:T(8,128)S(1)}, f32[4,64,128]{2,1,0:T(8,128)S(1)}, u32[]{:S(2)}, u32[]{:S(2)}) collective-permute-start(f32[4,64,128]{2,1,0:T(8,128)S(1)} %all-to-all-done.r0), channel_id=1, source_target_pairs={{0,12},{1,13},{2,14},{3,15},{4,0},{5,1},{6,2},{7,3},{8,4},{9,5},{1... | collective-permute-start | bytes 393224 | tf_op jit(solution)/shard_map/ppermute | solution.py:188
  35.0 9.3 %collective-permute-start = (f32[4,64,128]{2,1,0:T(8,128)S(1)}, f32[4,64,128]{2,1,0:T(8,128)S(1)}, u32[]{:S(2)}, u32[]{:S(2)}) collective-permute-start(f32[4,64,128]{2,1,0:T(8,128)S(1)} %all-to-all-done.r0), channel_id=1, source_target_pairs={{0,4},{1,5},{2,6},{3,7},{4,8},{5,9},{6,10},{7,11},{8,12},{9,13},{1... | collective-permute-start | bytes 393224 | tf_op jit(solution)/shard_map/ppermute | solution.py:188
  42.2 2.3 %copy-start.4 = (f32[4,64,128]{2,1,0:T(8,128)}, f32[4,64,128]{2,1,0:T(8,128)S(1)}, u32[]{:S(2)}) copy-start(f32[4,64,128]{2,1,0:T(8,128)S(1)} %collective-permute-done.2.r3) | copy-start | bytes 393220
  44.2 0.7 copy-start.5
  44.2 0.7 copy-start.6
  44.9 0.8 copy-start
  58.8 22.4 %all-to-all-start.3 = ((f32[8,2,64,128]{3,2,1,0:T(8,128)}), f32[8,2,64,128]{3,2,1,0:T(8,128)S(1)}, u32[]{:S(2)}, u32[]{:S(2)}) async-start(f32[8,2,64,128]{3,2,1,0:T(8,128)} %get-tuple-element.19), calls=%async_computation.3 | async-start | bytes 1048576 | tf_op jit(solution)/shard_map/all_to_all | solution.py:171
  63.2 9.8 %collective-permute-start.5 = (f32[4,64,128]{2,1,0:T(8,128)}, f32[4,64,128]{2,1,0:T(8,128)S(1)}, u32[]{:S(2)}, u32[]{:S(2)}) collective-permute-start(f32[4,64,128]{2,1,0:T(8,128)} %get-tuple-element.16), channel_id=1, source_target_pairs={{0,4},{1,5},{2,6},{3,7},{4,8},{5,9},{6,10},{7,11},{8,12},{9,13},{1... | collective-permute-start | bytes 393224 | tf_op jit(solution)/shard_map/ppermute | solution.py:188
  69.6 6.9 %collective-permute-start.6 = (f32[4,64,128]{2,1,0:T(8,128)}, f32[4,64,128]{2,1,0:T(8,128)S(1)}, u32[]{:S(2)}, u32[]{:S(2)}) collective-permute-start(f32[4,64,128]{2,1,0:T(8,128)} %get-tuple-element.17), channel_id=1, source_target_pairs={{0,12},{1,13},{2,14},{3,15},{4,0},{5,1},{6,2},{7,3},{8,4},{9,5},{1... | collective-permute-start | bytes 393224 | tf_op jit(solution)/shard_map/ppermute | solution.py:188
  69.6 9.9 %collective-permute-start.7 = (f32[4,64,128]{2,1,0:T(8,128)}, f32[4,64,128]{2,1,0:T(8,128)S(1)}, u32[]{:S(2)}, u32[]{:S(2)}) collective-permute-start(f32[4,64,128]{2,1,0:T(8,128)} %get-tuple-element.18), channel_id=1, source_target_pairs={{0,8},{1,9},{2,10},{3,11},{4,12},{5,13},{6,14},{7,15},{8,0},{9,1},... | collective-permute-start | bytes 393224 | tf_op jit(solution)/shard_map/ppermute | solution.py:188
  81.2 9.5 %all-to-all-start.2 = ((f32[4,64,128]{2,1,0:T(8,128)}), f32[4,64,128]{2,1,0:T(8,128)S(1)}, u32[]{:S(2)}, u32[]{:S(2)}) async-start(f32[4,64,128]{2,1,0:T(8,128)} %add_add_fusion.1), calls=%async_computation.2 | async-start | bytes 262144 | tf_op jit(solution)/shard_map/all_to_all | solution.py:171
  84.7 7.9 %collective-permute-start.8 = (f32[64,128]{1,0:T(8,128)S(1)}, f32[64,128]{1,0:T(8,128)S(1)}, u32[]{:S(2)}, u32[]{:S(2)}) collective-permute-start(f32[64,128]{1,0:T(8,128)S(1)} %slice_bitcast_fusion.4), channel_id=1, source_target_pairs={{0,128},{16,144},{32,160},{48,176},{64,192},{80,208},{96,224},{112... | collective-permute-start | bytes 98312 | tf_op jit(solution)/shard_map/ppermute | solution.py:184
  92.7 15.9 %collective-permute-start.9 = (f32[2,64,128]{2,1,0:T(8,128)S(1)}, f32[2,64,128]{2,1,0:T(8,128)S(1)}, u32[]{:S(2)}, u32[]{:S(2)}) collective-permute-start(f32[2,64,128]{2,1,0:T(8,128)S(1)} %pad_maximum_fusion.1), channel_id=1, source_target_pairs={{0,0},{1,16},{2,32},{3,48},{4,64},{5,80},{6,96},{7,112},{8,128},{9... | collective-permute-start | bytes 196616 | tf_op jit(solution)/shard_map/ppermute | solution.py:180
  109.3 11.2 %all-to-all-start.4 = ((f32[4,64,128]{2,1,0:T(8,128)}), f32[4,64,128]{2,1,0:T(8,128)S(1)}, u32[]{:S(2)}, u32[]{:S(2)}) async-start(f32[4,64,128]{2,1,0:T(8,128)} %broadcast_in_dim.14), calls=%async_computation.4 | async-start | bytes 262144 | tf_op jit(solution)/shard_map/all_to_all | solution.py:171
  112.6 7.9 %collective-permute-start.13 = (f32[64,128]{1,0:T(8,128)S(1)}, f32[64,128]{1,0:T(8,128)S(1)}, u32[]{:S(2)}, u32[]{:S(2)}) collective-permute-start(f32[64,128]{1,0:T(8,128)S(1)} %get-tuple-element.25), channel_id=1, source_target_pairs={{0,128},{16,144},{32,160},{48,176},{64,192},{80,208},{96,224},{112... | collective-permute-start | bytes 98312 | tf_op jit(solution)/shard_map/ppermute | solution.py:184
  120.5 14.8 %copy-start.3 = (f32[4,64,128]{2,1,0:T(8,128)}, f32[4,64,128]{2,1,0:T(8,128)S(1)}, u32[]{:S(2)}) copy-start(f32[4,64,128]{2,1,0:T(8,128)S(1)} %all-to-all-done.4.r0) | copy-start | bytes 393220
  121.4 13.9 %all-to-all-start.5 = ((f32[8,2,64,128]{3,2,1,0:T(8,128)}), f32[8,2,64,128]{3,2,1,0:T(8,128)S(1)}, u32[]{:S(2)}, u32[]{:S(2)}) async-start(f32[8,2,64,128]{3,2,1,0:T(8,128)} %broadcast_in_dim.15), calls=%async_computation.5 | async-start | bytes 1048576 | tf_op jit(solution)/shard_map/all_to_all | solution.py:171
  125.0 7.9 %collective-permute-start.12 = (f32[4,64,128]{2,1,0:T(8,128)S(1)}, f32[4,64,128]{2,1,0:T(8,128)S(1)}, u32[]{:S(2)}, u32[]{:S(2)}) collective-permute-start(f32[4,64,128]{2,1,0:T(8,128)S(1)} %all-to-all-done.4.r0), channel_id=1, source_target_pairs={{0,8},{1,9},{2,10},{3,11},{4,12},{5,13},{6,14},{7,15},{8,0},{9,1},... | collective-permute-start | bytes 393224 | tf_op jit(solution)/shard_map/ppermute | solution.py:188
  125.0 9.9 %collective-permute-start.11 = (f32[4,64,128]{2,1,0:T(8,128)S(1)}, f32[4,64,128]{2,1,0:T(8,128)S(1)}, u32[]{:S(2)}, u32[]{:S(2)}) collective-permute-start(f32[4,64,128]{2,1,0:T(8,128)S(1)} %all-to-all-done.4.r0), channel_id=1, source_target_pairs={{0,12},{1,13},{2,14},{3,15},{4,0},{5,1},{6,2},{7,3},{8,4},{9,5},{1... | collective-permute-start | bytes 393224 | tf_op jit(solution)/shard_map/ppermute | solution.py:188
  126.3 8.6 %collective-permute-start.10 = (f32[4,64,128]{2,1,0:T(8,128)S(1)}, f32[4,64,128]{2,1,0:T(8,128)S(1)}, u32[]{:S(2)}, u32[]{:S(2)}) collective-permute-start(f32[4,64,128]{2,1,0:T(8,128)S(1)} %all-to-all-done.4.r0), channel_id=1, source_target_pairs={{0,4},{1,5},{2,6},{3,7},{4,8},{5,9},{6,10},{7,11},{8,12},{9,13},{1... | collective-permute-start | bytes 393224 | tf_op jit(solution)/shard_map/ppermute | solution.py:188
  132.9 2.5 %copy-start.7 = (f32[4,64,128]{2,1,0:T(8,128)}, f32[4,64,128]{2,1,0:T(8,128)S(1)}, u32[]{:S(2)}) copy-start(f32[4,64,128]{2,1,0:T(8,128)S(1)} %collective-permute-done.12.r3) | copy-start | bytes 393220
  134.9 0.7 copy-start.8
  134.9 0.7 copy-start.9
  135.6 0.8 copy-start.1
  149.4 14.8 %all-to-all-start.7 = ((f32[8,2,64,128]{3,2,1,0:T(8,128)}), f32[8,2,64,128]{3,2,1,0:T(8,128)S(1)}, u32[]{:S(2)}, u32[]{:S(2)}) async-start(f32[8,2,64,128]{3,2,1,0:T(8,128)} %get-tuple-element.24), calls=%async_computation.7 | async-start | bytes 1048576 | tf_op jit(solution)/shard_map/all_to_all | solution.py:171
  153.8 19.4 %collective-permute-start.14 = (f32[4,64,128]{2,1,0:T(8,128)}, f32[4,64,128]{2,1,0:T(8,128)S(1)}, u32[]{:S(2)}, u32[]{:S(2)}) collective-permute-start(f32[4,64,128]{2,1,0:T(8,128)} %get-tuple-element.21), channel_id=1, source_target_pairs={{0,4},{1,5},{2,6},{3,7},{4,8},{5,9},{6,10},{7,11},{8,12},{9,13},{1... | collective-permute-start | bytes 393224 | tf_op jit(solution)/shard_map/ppermute | solution.py:188
  160.5 12.8 %collective-permute-start.15 = (f32[4,64,128]{2,1,0:T(8,128)}, f32[4,64,128]{2,1,0:T(8,128)S(1)}, u32[]{:S(2)}, u32[]{:S(2)}) collective-permute-start(f32[4,64,128]{2,1,0:T(8,128)} %get-tuple-element.22), channel_id=1, source_target_pairs={{0,12},{1,13},{2,14},{3,15},{4,0},{5,1},{6,2},{7,3},{8,4},{9,5},{1... | collective-permute-start | bytes 393224 | tf_op jit(solution)/shard_map/ppermute | solution.py:188
  160.5 12.8 %collective-permute-start.16 = (f32[4,64,128]{2,1,0:T(8,128)}, f32[4,64,128]{2,1,0:T(8,128)S(1)}, u32[]{:S(2)}, u32[]{:S(2)}) collective-permute-start(f32[4,64,128]{2,1,0:T(8,128)} %get-tuple-element.23), channel_id=1, source_target_pairs={{0,8},{1,9},{2,10},{3,11},{4,12},{5,13},{6,14},{7,15},{8,0},{9,1},... | collective-permute-start | bytes 393224 | tf_op jit(solution)/shard_map/ppermute | solution.py:188
  164.2 14.5 %collective-permute-start.17 = (f32[64,128]{1,0:T(8,128)S(1)}, f32[64,128]{1,0:T(8,128)S(1)}, u32[]{:S(2)}, u32[]{:S(2)}) collective-permute-start(f32[64,128]{1,0:T(8,128)S(1)} %slice_bitcast_fusion), channel_id=1, source_target_pairs={{0,128},{16,144},{32,160},{48,176},{64,192},{80,208},{96,224},{112... | collective-permute-start | bytes 98312 | tf_op jit(solution)/shard_map/ppermute | solution.py:184
  174.9 9.8 %all-to-all-start.6 = ((f32[4,64,128]{2,1,0:T(8,128)}), f32[4,64,128]{2,1,0:T(8,128)S(1)}, u32[]{:S(2)}, u32[]{:S(2)}) async-start(f32[4,64,128]{2,1,0:T(8,128)} %add_add_fusion), calls=%async_computation.6 | async-start | bytes 262144 | tf_op jit(solution)/shard_map/all_to_all | solution.py:171
  178.8 14.2 %collective-permute-start.18 = (f32[64,128]{1,0:T(8,128)S(1)}, f32[64,128]{1,0:T(8,128)S(1)}, u32[]{:S(2)}, u32[]{:S(2)}) collective-permute-start(f32[64,128]{1,0:T(8,128)S(1)} %fusion), channel_id=1, source_target_pairs={{0,0},{1,16},{2,32},{3,48},{4,64},{5,80},{6,96},{7,112},{8,128},{9... | collective-permute-start | bytes 98312 | tf_op jit(solution)/shard_map/ppermute | solution.py:180

commit v3 on v2

v3 whole, which is shorter than its diff:
```python
import jax
import jax.numpy as jnp
from jax import lax
from jax.experimental import pallas as pl
from jax.experimental.pallas import tpu as pltpu
from jax.sharding import PartitionSpec as P

ITERS = 2
DIMS = 64
PIECE = 128
CHUNK = 256
TALL = 512
WIDE = 512
HALF = 4
STEPS = 4
BLOCK = 8
STACK = 3 * DIMS + 16
SAMPLES = 32768

Z_GROUPS = [[4 * x + z for z in range(4)] for x in range(4)]
YC_GROUPS = [list(range(8)), list(range(8, 16))]
SHIFTS = (1, 3, 2)


def nn(a, b):
    return lax.dot_general(a, b, (((1,), (0,)), ((), ())), preferred_element_type=jnp.float32)


def tile_kernel(
    where_ref, values_hbm, *refs,
):
    sources, targets = refs[:5], refs[5:10]
    (given, made), (given_cols, made_cols) = refs[10:12], refs[12:14]
    values_ref, left, right, stack, table, norm_i, norm_j, acc, acc_lead, value_sem, coord_sem, term_sem = refs[14:]
    lead_base, trail_base, diagonal = where_ref[0], where_ref[1], where_ref[2]
    x_pos, z_pos = where_ref[3], where_ref[4]

    def at(n, length=CHUNK):
        return pl.ds(pl.multiple_of(n * CHUNK, CHUNK), length)

    def band(step):
        return pl.ds(pl.multiple_of(step * TALL, TALL), TALL)

    def value_copy(step):
        return pltpu.make_async_copy(values_hbm.at[band(step)], values_ref.at[band(step)], value_sem.at[step])

    def row_group(t, send):
        shift = (0, *SHIFTS)[t]
        return lax.rem(x_pos + (shift if send else 4 - shift), 4)

    coord_copies = [pltpu.make_async_copy(sources[t], given.at[row_group(t, False)], coord_sem.at[t]) for t in range(4)]
    coord_copies.append(pltpu.make_async_copy(sources[4], given_cols, coord_sem.at[4]))
    term_copies = [pltpu.make_async_copy(made.at[row_group(t, True)], targets[t], term_sem.at[t]) for t in range(4)]
    term_copies.append(pltpu.make_async_copy(made_cols, targets[4], term_sem.at[4]))

    for copy in coord_copies:
        copy.start()
    for step in range(STEPS):
        value_copy(step).start()
    acc[...] = jnp.zeros_like(acc)
    acc_lead[...] = jnp.zeros_like(acc_lead)
    for copy in coord_copies:
        copy.wait()

    def places():
        for n in range(BLOCK):
            yield n, given.at[n // 2, n % 2 * 2], given.at[n // 2, n % 2 * 2 + 1], made.at[n // 2, n % 2 * 2], made.at[n // 2, n % 2 * 2 + 1]
        for s in range(2):
            half = z_pos if s == 0 else 1 - z_pos
            for m in range(4):
                n = BLOCK + 4 * half + m
                yield n, given_cols.at[2 * m, s], given_cols.at[2 * m + 1, s], made_cols.at[2 * m, s], made_cols.at[2 * m + 1, s]

    for n, a, b, _, _ in places():
        def split():
            x = jnp.concatenate([a[...], b[...]], axis=1)
            hi = x.astype(jnp.bfloat16)
            hi32 = hi.astype(jnp.float32)
            rest = x - hi32
            mid = rest.astype(jnp.bfloat16)
            mid32 = mid.astype(jnp.float32)
            lo = (rest - mid32).astype(jnp.bfloat16)
            near = hi32 + mid32
            norms = jnp.sum(near * near, axis=0, keepdims=True)
            main = jnp.concatenate([hi32, mid32], axis=0).T.astype(jnp.bfloat16)
            return hi, mid, lo, norms, main

        @pl.when(jnp.logical_and(n >= lead_base, n < lead_base + BLOCK))
        def _():
            hi, mid, lo, norms, main = split()
            stack[:, at(n)] = jnp.concatenate([hi, mid, lo, jnp.ones((16, CHUNK), jnp.bfloat16)], axis=0)
            left[at(n), :] = jnp.concatenate([main, main], axis=1)
            norm_i[at(n), :] = jnp.broadcast_to(norms, (PIECE, CHUNK)).T

        @pl.when(jnp.logical_and(n >= trail_base, n < trail_base + jnp.where(diagonal == 1, BLOCK, HALF)))
        def _():
            hi, mid, lo, norms, main = split()
            right[:, at(n)] = -2.0 * jnp.concatenate([hi, mid, mid, hi], axis=0)
            lo32 = lo.astype(jnp.float32)
            tail = jnp.concatenate([lo32, jnp.ones_like(lo32)], axis=0).T.astype(jnp.bfloat16)
            table[at(n), :] = jnp.concatenate([main, tail], axis=1)
            norm_j[:, at(n)] = jnp.broadcast_to(norms + 1.0, (8, CHUNK))

    def ratios_of(values, lead, trail):
        inner = nn(left[at(lead, TALL), :], right[:, at(trail, WIDE)])
        ni = jnp.concatenate([norm_i[at(lead, TALL), :]] * (WIDE // PIECE), axis=1)
        squared = inner + (ni + norm_j[0:1, at(trail, WIDE)])
        return values * lax.rsqrt(squared)

    def products(ratios, lead, trail):
        hi = ratios.astype(jnp.bfloat16)
        lo = (ratios - hi.astype(jnp.float32)).astype(jnp.bfloat16)
        above, beside = stack[:, at(lead, TALL)], table[at(trail, WIDE), :]
        acc[:, at(trail, WIDE)] += nn(above, hi) + nn(above, lo)
        acc_lead[at(lead - lead_base, TALL), :] += nn(hi, beside) + nn(lo, beside)

    def values_at(step, j):
        return values_ref[band(step), pl.ds(pl.multiple_of(j * WIDE, WIDE), WIDE)]

    @pl.loop(0, STEPS)
    def _(step):
        value_copy(step).wait()
        special = jnp.logical_and(diagonal == 1, step < 2)

        @pl.when(jnp.logical_not(special))
        def _():
            lead = lead_base + 2 * step
            for j in range(2):
                trail = trail_base + 2 * j
                products(ratios_of(values_at(step, j), lead, trail), lead, trail)

        @pl.when(special)
        def _():
            @pl.loop(0, 3)
            def _(k):
                late = jnp.logical_or(k == 2, jnp.logical_and(step == 1, k == 1)).astype(jnp.int32)
                j = jnp.where(step == 0, k % 2, jnp.where(k == 1, 0, 1))
                row_iota = lax.broadcasted_iota(jnp.int32, (TALL, WIDE), 0) + step * TALL
                col_iota = lax.broadcasted_iota(jnp.int32, (TALL, WIDE), 1) + j * WIDE
                keep = (col_iota - row_iota) * (1 - 2 * late) > 0
                lead, trail = 2 * step + HALF * late, 2 * j + HALF * late
                ratios = jnp.where(keep, ratios_of(values_at(step, j), lead, trail), 0.0)
                products(ratios, lead, trail)

    for n in range(BLOCK):
        acc[:, at(lead_base + n)] += acc_lead[n * CHUNK : (n + 1) * CHUNK, :].T[:STACK]
    for k, (n, a, b, c, d) in enumerate(places()):
        x = jnp.concatenate([a[...], b[...]], axis=1)
        part = acc[:, at(n)]
        pulled = part[0:DIMS] + part[DIMS : 2 * DIMS] + part[2 * DIMS : 3 * DIMS]
        terms = x * part[3 * DIMS : 3 * DIMS + 1] - pulled
        c[...] = terms[:, :PIECE]
        d[...] = terms[:, PIECE:]
        if k == BLOCK - 1:
            for copy in term_copies[:4]:
                copy.start()
    term_copies[4].start()
    for copy in term_copies:
        copy.wait()


def tile_terms(where, values, groups, cols):
    row_shape = jax.ShapeDtypeStruct(groups[0].shape, jnp.float32)
    col_shape = jax.ShapeDtypeStruct(cols.shape, jnp.float32)
    total = 2 * BLOCK * CHUNK
    anywhere = pl.BlockSpec(memory_space=pl.ANY)
    rows_buffer = pltpu.VMEM((4, *groups[0].shape), jnp.float32)
    cols_buffer = pltpu.VMEM(cols.shape, jnp.float32)
    return pl.pallas_call(
        tile_kernel,
        out_shape=(row_shape,) * 4 + (col_shape,),
        in_specs=[pl.BlockSpec(memory_space=pltpu.SMEM)] + [anywhere] * 6,
        out_specs=(anywhere,) * 5,
        scratch_shapes=[
            rows_buffer, rows_buffer, cols_buffer, cols_buffer,
            pltpu.VMEM(values.shape, jnp.float32),
            pltpu.VMEM((total, CHUNK), jnp.bfloat16),
            pltpu.VMEM((CHUNK, total), jnp.bfloat16),
            pltpu.VMEM((STACK, total), jnp.bfloat16),
            pltpu.VMEM((total, CHUNK), jnp.bfloat16),
            pltpu.VMEM((total, PIECE), jnp.float32),
            pltpu.VMEM((8, total), jnp.float32),
            pltpu.VMEM((STACK, total), jnp.float32),
            pltpu.VMEM((total // 2, CHUNK), jnp.float32),
            pltpu.SemaphoreType.DMA((STEPS,)),
            pltpu.SemaphoreType.DMA((5,)),
            pltpu.SemaphoreType.DMA((5,)),
        ],
        compiler_params=pltpu.CompilerParams(vmem_limit_bytes=48 * 1024 * 1024),
        cost_estimate=pl.CostEstimate(flops=6_000_000_000, transcendentals=2_097_152, bytes_accessed=10_000_000),
    )(where, values, *groups, cols)


def exchange(x, axis, groups):
    return lax.all_to_all(x, axis, split_axis=0, concat_axis=0, tiled=True, axis_index_groups=groups)


def spread(x, axis, groups):
    return exchange(jnp.broadcast_to(x, (len(groups[0]), *x.shape)), axis, groups)


def transposed(x):
    pairs = [(a * 16 + b, b * 16 + a) for a in range(16) for b in range(16)]
    return lax.ppermute(x, ("row", "col"), pairs)


def across(x):
    return lax.ppermute(x, "row", [(a, (a + 8) % 16) for a in range(16)])


def along(x, shift):
    return lax.ppermute(x, "col", [(a, (a + 4 * shift) % 16) for a in range(16)])


def gathered(own, turned):
    line = spread(own, "col", Z_GROUPS)
    other = across(turned)
    cols = spread(jnp.stack([turned, other]), "row", YC_GROUPS)
    return (line, *(along(line, s) for s in SHIFTS)), cols


def reduced(groups, cols):
    kept, sent = exchange(cols, "row", YC_GROUPS).sum(axis=0)
    line = groups[0]
    for part, s in zip(groups[1:], SHIFTS):
        line = line + along(part, s)
    came = across(sent)
    row_sum = exchange(line, "col", Z_GROUPS).sum(axis=0)
    return row_sum, kept + came


def local(coords, dissimilarity):
    row, col = lax.axis_index("row"), lax.axis_index("col")
    lead_base = jnp.where(row > col, BLOCK, 0)
    trail_base = jnp.where(row < col, BLOCK, jnp.where(row > col, HALF, 0))
    diagonal = (row == col).astype(jnp.int32)
    where = jnp.stack([lead_base, trail_base, diagonal, col // 4, row // 8]).astype(jnp.int32)
    own, turned = coords, transposed(coords)
    scale = 1.0 / SAMPLES
    for iteration in range(ITERS):
        groups, cols = gathered(own, turned)
        *groups, cols = tile_terms(where, dissimilarity, groups, cols)
        row_sum, col_sum = reduced(groups, cols)
        if iteration + 1 < ITERS:
            came = transposed(jnp.stack([row_sum, col_sum]))
            own = (row_sum + came[1]) * scale
            turned = (col_sum + came[0]) * scale
        else:
            own = (row_sum + transposed(col_sum)) * scale
    return own


def solution(mesh):
    in_specs = (P(None, ("row", "col")), P("row", "col"))
    out_specs = P(None, ("row", "col"))
    return jax.shard_map(local, mesh=mesh, in_specs=in_specs, out_specs=out_specs, check_vma=False)
```

time: 195 us -> 184 us (0.944)
  starting transfers between devices: 94.6 us -> 86.5 us
  waiting for transfers between devices: 62.2 us -> 65.3 us
  local copies, waits for them, and re-layouts: 6.75 us -> 3.87 us
    ppermute x12, starting transfers between devices: 25.5 us -> 20.5 us  [along(): lax.ppermute(x, 'col', [(a, (a + 4 * shift) % 16) for a in range(16)])]
    all_to_all x8, waiting for transfers between devices: 5.29 us -> 8 us  [exchange(): lax.all_to_all(x, axis, split_axis=0, concat_axis=0, tiled=True, axis_ind...]
    ppermute x4, starting transfers between devices: 13.5 us -> 11 us  [across(): return lax.ppermute(x, 'row', [(a, (a + 8) % 16) for a in range(16)])]
    unnamed x20 -> x0, local copies, waits for them, and re-layouts: 2.29 us -> none
  transfers between devices with their start and end apart: 27 -> 27, of which waited for: 17 -> 17; matrix products, arithmetic and copies ran while one was open for 2% -> 1% of each run, Pallas kernels for 0% -> 0%
where the time goes in v3:
time: 184 us; the launch traced here: 183 us
  starting transfers between devices  86.5 us (47%)
  waiting for transfers between devices  65.3 us (35%)
  Pallas kernels  24.9 us (14%)
  local copies, waits for them, and re-layouts  3.87 us (2%)
  other arithmetic  2.13 us (1%)
    all_to_all x8, starting transfers between devices, exchange(): lax.all_to_all(x, axis, split_axis=0, concat_axis=0, tiled=True, axis_ind...  32.1 us
    pallas_call x2, Pallas kernels, tile_terms(): pl.pallas_call(tile_kernel, out_shape=(row_shape,) * 4 + (col_shape,), in...  24.9 us
    ppermute x3, starting transfers between devices, transposed(): return lax.ppermute(x, ('row', 'col'), pairs)  22.9 us
    ppermute x3, waiting for transfers between devices, transposed(): return lax.ppermute(x, ('row', 'col'), pairs)  20.6 us
    ppermute x12, starting transfers between devices, along(): lax.ppermute(x, 'col', [(a, (a + 4 * shift) % 16) for a in range(16)])  20.5 us
    ppermute x12, waiting for transfers between devices, along(): lax.ppermute(x, 'col', [(a, (a + 4 * shift) % 16) for a in range(16)])  19.4 us
    ppermute x4, waiting for transfers between devices, across(): return lax.ppermute(x, 'row', [(a, (a + 8) % 16) for a in range(16)])  17.2 us
    ppermute x4, starting transfers between devices, across(): return lax.ppermute(x, 'row', [(a, (a + 8) % 16) for a in range(16)])  11 us
  transfers between devices with their start and end apart: 27, of which 17 were waited for; matrix products, arithmetic and copies ran while one was open for 1% of the time, Pallas kernels for 0%

profile of v3, /device:TPU:6, one launch (start us, length us, event | category | flops | bytes accessed | tf_op | source)
XLA Modules:
  0.0 182.9 jit_solution(15335371945785643916)
XLA Ops:
  0.0 1.4 broadcast_in_dim.12
  1.4 5.9 %all-to-all-start = ((f32[4,64,128]{2,1,0:T(8,128)}), f32[4,64,128]{2,1,0:T(8,128)S(1)}, u32[]{:S(2)}, u32[]{:S(2)}) async-start(f32[4,64,128]{2,1,0:T(8,128)} %broadcast_in_dim.12), calls=%async_computation | async-start | bytes 262144 | tf_op jit(solution)/shard_map/all_to_all | solution.py:195
  7.3 9.1 %collective-permute-start.3 = (f32[64,128]{1,0:T(8,128)}, f32[64,128]{1,0:T(8,128)S(1)}, u32[]{:S(2)}, u32[]{:S(2)}) collective-permute-start(f32[64,128]{1,0:T(8,128)} %param.2), channel_id=1, source_target_pairs={{0,0},{1,16},{2,32},{3,48},{4,64},{5,80},{6,96},{7,112},{8,128},{9... | collective-permute-start | bytes 98312 | tf_op jit(solution)/shard_map/ppermute | solution.py:204
  16.4 5.3 %collective-permute-done.3 = f32[64,128]{1,0:T(8,128)S(1)} collective-permute-done((f32[64,128]{1,0:T(8,128)}, f32[64,128]{1,0:T(8,128)S(1)}, u32[]{:S(2)}, u32[]{:S(2)}) %collective-permute-start.3) | collective-permute-done | bytes 32800 | tf_op jit(solution)/shard_map/ppermute | solution.py:204
  21.7 0.0 collective-permute-start.4
  21.7 8.2 %collective-permute-done.4 = f32[64,128]{1,0:T(8,128)S(1)} collective-permute-done((f32[64,128]{1,0:T(8,128)S(1)}, f32[64,128]{1,0:T(8,128)S(1)}, u32[]{:S(2)}, u32[]{:S(2)}) %collective-permute-start.4) | collective-permute-done | bytes 32800 | tf_op jit(solution)/shard_map/ppermute | solution.py:208
  29.9 0.0 all-to-all-done.refs_0_
  29.9 0.9 broadcast_in_dim.13
  30.8 3.5 %all-to-all-start.1 = ((f32[8,2,64,128]{3,2,1,0:T(8,128)}), f32[8,2,64,128]{3,2,1,0:T(8,128)S(1)}, u32[]{:S(2)}, u32[]{:S(2)}) async-start(f32[8,2,64,128]{3,2,1,0:T(8,128)} %broadcast_in_dim.13), calls=%async_computation.1 | async-start | bytes 1048576 | tf_op jit(solution)/shard_map/all_to_all | solution.py:195
  34.3 0.1 collective-permute-start.2
  34.4 0.6 collective-permute-start.1
  35.0 2.7 %collective-permute-start = (f32[4,64,128]{2,1,0:T(8,128)S(1)}, f32[4,64,128]{2,1,0:T(8,128)S(1)}, u32[]{:S(2)}, u32[]{:S(2)}) collective-permute-start(f32[4,64,128]{2,1,0:T(8,128)S(1)} %all-to-all-done.refs_0_), channel_id=1, source_target_pairs={{0,4},{1,5},{2,6},{3,7},{4,8},{5,9},{6,10},{7,11},{8,12},{9,13},{1... | collective-permute-start | bytes 393224 | tf_op jit(solution)/shard_map/ppermute | solution.py:212
  37.7 0.1 stack.54.where_ref
  37.8 4.5 %collective-permute-done.2.refs_3_ = f32[4,64,128]{2,1,0:T(8,128)S(1)} collective-permute-done((f32[4,64,128]{2,1,0:T(8,128)S(1)}, f32[4,64,128]{2,1,0:T(8,128)S(1)}, u32[]{:S(2)}, u32[]{:S(2)}) %collective-permute-start.2) | collective-permute-done | bytes 131104 | tf_op jit(solution)/shard_map/ppermute | solution.py:212
  42.2 2.0 %collective-permute-done.1.refs_2_ = f32[4,64,128]{2,1,0:T(8,128)S(1)} collective-permute-done((f32[4,64,128]{2,1,0:T(8,128)S(1)}, f32[4,64,128]{2,1,0:T(8,128)S(1)}, u32[]{:S(2)}, u32[]{:S(2)}) %collective-permute-start.1) | collective-permute-done | bytes 131104 | tf_op jit(solution)/shard_map/ppermute | solution.py:212
  44.2 0.0 collective-permute-done.refs_1_
  44.2 0.3 all-to-all-done.1.refs_4_
  44.5 12.5 %shard_map.28 = (f32[4,64,128]{2,1,0:T(8,128)S(1)}, f32[4,64,128]{2,1,0:T(8,128)S(1)}, f32[4,64,128]{2,1,0:T(8,128)S(1)}, f32[4,64,128]{2,1,0:T(8,128)S(1)}, f32[8,2,64,128]{3,2,1,0:T(8,128)}) custom-call(s32[5]{0:T(128)S(1)} %stack.54.where_ref, f32[2048,1024]{1,0:T(8,128)} %values_hbm.3, f32[4,64,128]{2,1,0:T(8,128)S(1)} %all-to-all-done.refs_0_, ...), custom_call_target="tpu_custom_call" | custom-call | flops 6000000000 | bytes 10000000 | tf_op jit(solution)/shard_map/pallas_call | solution.py:169
  57.0 4.2 %all-to-all-start.3 = ((f32[8,2,64,128]{3,2,1,0:T(8,128)}), f32[8,2,64,128]{3,2,1,0:T(8,128)S(1)}, u32[]{:S(2)}, u32[]{:S(2)}) async-start(f32[8,2,64,128]{3,2,1,0:T(8,128)} %get-tuple-element.19), calls=%async_computation.3 | async-start | bytes 1048576 | tf_op jit(solution)/shard_map/all_to_all | solution.py:195
  61.2 3.7 %collective-permute-start.5 = (f32[4,64,128]{2,1,0:T(8,128)S(1)}, f32[4,64,128]{2,1,0:T(8,128)S(1)}, u32[]{:S(2)}, u32[]{:S(2)}) collective-permute-start(f32[4,64,128]{2,1,0:T(8,128)S(1)} %get-tuple-element.16), channel_id=1, source_target_pairs={{0,4},{1,5},{2,6},{3,7},{4,8},{5,9},{6,10},{7,11},{8,12},{9,13},{1... | collective-permute-start | bytes 393224 | tf_op jit(solution)/shard_map/ppermute | solution.py:212
  64.9 0.0 collective-permute-start.6
  64.9 3.6 %collective-permute-start.7 = (f32[4,64,128]{2,1,0:T(8,128)S(1)}, f32[4,64,128]{2,1,0:T(8,128)S(1)}, u32[]{:S(2)}, u32[]{:S(2)}) collective-permute-start(f32[4,64,128]{2,1,0:T(8,128)S(1)} %get-tuple-element.18), channel_id=1, source_target_pairs={{0,8},{1,9},{2,10},{3,11},{4,12},{5,13},{6,14},{7,15},{8,0},{9,1},... | collective-permute-start | bytes 393224 | tf_op jit(solution)/shard_map/ppermute | solution.py:212
  68.5 0.0 collective-permute-done.5
  68.5 3.3 %collective-permute-done.6 = f32[4,64,128]{2,1,0:T(8,128)S(1)} collective-permute-done((f32[4,64,128]{2,1,0:T(8,128)S(1)}, f32[4,64,128]{2,1,0:T(8,128)S(1)}, u32[]{:S(2)}, u32[]{:S(2)}) %collective-permute-start.6) | collective-permute-done | bytes 131104 | tf_op jit(solution)/shard_map/ppermute | solution.py:212
  71.8 3.1 %collective-permute-done.7 = f32[4,64,128]{2,1,0:T(8,128)S(1)} collective-permute-done((f32[4,64,128]{2,1,0:T(8,128)S(1)}, f32[4,64,128]{2,1,0:T(8,128)S(1)}, u32[]{:S(2)}, u32[]{:S(2)}) %collective-permute-start.7) | collective-permute-done | bytes 131104 | tf_op jit(solution)/shard_map/ppermute | solution.py:212
  74.9 0.7 add_add_fusion.1
  75.6 0.0 all-to-all-done.3
  75.6 3.7 %all-to-all-start.2 = ((f32[4,64,128]{2,1,0:T(8,128)}), f32[4,64,128]{2,1,0:T(8,128)S(1)}, u32[]{:S(2)}, u32[]{:S(2)}) async-start(f32[4,64,128]{2,1,0:T(8,128)} %add_add_fusion.1), calls=%async_computation.2 | async-start | bytes 262144 | tf_op jit(solution)/shard_map/all_to_all | solution.py:195
  79.4 3.6 %collective-permute-start.8 = (f32[64,128]{1,0:T(8,128)S(1)}, f32[64,128]{1,0:T(8,128)S(1)}, u32[]{:S(2)}, u32[]{:S(2)}) collective-permute-start(f32[64,128]{1,0:T(8,128)S(1)} %slice_bitcast_fusion.4), channel_id=1, source_target_pairs={{0,128},{16,144},{32,160},{48,176},{64,192},{80,208},{96,224},{112... | collective-permute-start | bytes 98312 | tf_op jit(solution)/shard_map/ppermute | solution.py:208
  83.0 2.3 %all-to-all-done.2 = f32[4,64,128]{2,1,0:T(8,128)S(1)} async-done(((f32[4,64,128]{2,1,0:T(8,128)}), f32[4,64,128]{2,1,0:T(8,128)S(1)}, u32[]{:S(2)}, u32[]{:S(2)}) %all-to-all-start.2) | async-done | bytes 131104 | tf_op jit(solution)/shard_map/all_to_all | solution.py:195
  85.3 2.0 %collective-permute-done.8 = f32[64,128]{1,0:T(8,128)S(1)} collective-permute-done((f32[64,128]{1,0:T(8,128)S(1)}, f32[64,128]{1,0:T(8,128)S(1)}, u32[]{:S(2)}, u32[]{:S(2)}) %collective-permute-start.8) | collective-permute-done | bytes 32800 | tf_op jit(solution)/shard_map/ppermute | solution.py:208
  87.3 8.9 %collective-permute-start.9 = (f32[2,64,128]{2,1,0:T(8,128)S(1)}, f32[2,64,128]{2,1,0:T(8,128)S(1)}, u32[]{:S(2)}, u32[]{:S(2)}) collective-permute-start(f32[2,64,128]{2,1,0:T(8,128)S(1)} %pad_maximum_fusion.1), channel_id=1, source_target_pairs={{0,0},{1,16},{2,32},{3,48},{4,64},{5,80},{6,96},{7,112},{8,128},{9... | collective-permute-start | bytes 196616 | tf_op jit(solution)/shard_map/ppermute | solution.py:204
  96.2 7.0 %collective-permute-done.9 = f32[2,64,128]{2,1,0:T(8,128)S(1)} collective-permute-done((f32[2,64,128]{2,1,0:T(8,128)S(1)}, f32[2,64,128]{2,1,0:T(8,128)S(1)}, u32[]{:S(2)}, u32[]{:S(2)}) %collective-permute-start.9) | collective-permute-done | bytes 65568 | tf_op jit(solution)/shard_map/ppermute | solution.py:204
  103.2 0.7 broadcast_in_dim.14
  103.9 3.3 %all-to-all-start.4 = ((f32[4,64,128]{2,1,0:T(8,128)}), f32[4,64,128]{2,1,0:T(8,128)S(1)}, u32[]{:S(2)}, u32[]{:S(2)}) async-start(f32[4,64,128]{2,1,0:T(8,128)} %broadcast_in_dim.14), calls=%async_computation.4 | async-start | bytes 262144 | tf_op jit(solution)/shard_map/all_to_all | solution.py:195
  107.2 0.8 collective-permute-start.13
  108.0 7.1 %collective-permute-done.13 = f32[64,128]{1,0:T(8,128)S(1)} collective-permute-done((f32[64,128]{1,0:T(8,128)S(1)}, f32[64,128]{1,0:T(8,128)S(1)}, u32[]{:S(2)}, u32[]{:S(2)}) %collective-permute-start.13) | collective-permute-done | bytes 32800 | tf_op jit(solution)/shard_map/ppermute | solution.py:208
  115.1 0.0 all-to-all-done.4.refs_0_
  115.1 0.9 broadcast_in_dim.15
  116.0 3.6 %all-to-all-start.5 = ((f32[8,2,64,128]{3,2,1,0:T(8,128)}), f32[8,2,64,128]{3,2,1,0:T(8,128)S(1)}, u32[]{:S(2)}, u32[]{:S(2)}) async-start(f32[8,2,64,128]{3,2,1,0:T(8,128)} %broadcast_in_dim.15), calls=%async_computation.5 | async-start | bytes 1048576 | tf_op jit(solution)/shard_map/all_to_all | solution.py:195
  119.6 0.0 collective-permute-start.12
  119.6 1.3 collective-permute-start.11
  120.9 2.1 %collective-permute-start.10 = (f32[4,64,128]{2,1,0:T(8,128)S(1)}, f32[4,64,128]{2,1,0:T(8,128)S(1)}, u32[]{:S(2)}, u32[]{:S(2)}) collective-permute-start(f32[4,64,128]{2,1,0:T(8,128)S(1)} %all-to-all-done.4.refs_0_), channel_id=1, source_target_pairs={{0,4},{1,5},{2,6},{3,7},{4,8},{5,9},{6,10},{7,11},{8,12},{9,13},{1... | collective-permute-start | bytes 393224 | tf_op jit(solution)/shard_map/ppermute | solution.py:212
  123.0 4.5 %collective-permute-done.12.refs_3_ = f32[4,64,128]{2,1,0:T(8,128)S(1)} collective-permute-done((f32[4,64,128]{2,1,0:T(8,128)S(1)}, f32[4,64,128]{2,1,0:T(8,128)S(1)}, u32[]{:S(2)}, u32[]{:S(2)}) %collective-permute-start.12) | collective-permute-done | bytes 131104 | tf_op jit(solution)/shard_map/ppermute | solution.py:212
  127.5 2.0 %collective-permute-done.11.refs_2_ = f32[4,64,128]{2,1,0:T(8,128)S(1)} collective-permute-done((f32[4,64,128]{2,1,0:T(8,128)S(1)}, f32[4,64,128]{2,1,0:T(8,128)S(1)}, u32[]{:S(2)}, u32[]{:S(2)}) %collective-permute-start.11) | collective-permute-done | bytes 131104 | tf_op jit(solution)/shard_map/ppermute | solution.py:212
  129.5 0.0 collective-permute-done.10.refs_1_
  129.5 0.4 all-to-all-done.5.refs_4_
  129.9 12.5 %shard_map.29 = (f32[4,64,128]{2,1,0:T(8,128)S(1)}, f32[4,64,128]{2,1,0:T(8,128)S(1)}, f32[4,64,128]{2,1,0:T(8,128)S(1)}, f32[4,64,128]{2,1,0:T(8,128)S(1)}, f32[8,2,64,128]{3,2,1,0:T(8,128)}) custom-call(s32[5]{0:T(128)S(1)} %stack.54.where_ref, f32[2048,1024]{1,0:T(8,128)} %values_hbm.3, f32[4,64,128]{2,1,0:T(8,128)S(1)} %all-to-all-done.4.refs_0_, ...), custom_call_target="tpu_custom_call" | custom-call | flops 6000000000 | bytes 10000000 | tf_op jit(solution)/shard_map/pallas_call | solution.py:169
  142.4 4.1 %all-to-all-start.7 = ((f32[8,2,64,128]{3,2,1,0:T(8,128)}), f32[8,2,64,128]{3,2,1,0:T(8,128)S(1)}, u32[]{:S(2)}, u32[]{:S(2)}) async-start(f32[8,2,64,128]{3,2,1,0:T(8,128)} %get-tuple-element.24), calls=%async_computation.7 | async-start | bytes 1048576 | tf_op jit(solution)/shard_map/all_to_all | solution.py:195
  146.5 3.9 %collective-permute-start.14 = (f32[4,64,128]{2,1,0:T(8,128)S(1)}, f32[4,64,128]{2,1,0:T(8,128)S(1)}, u32[]{:S(2)}, u32[]{:S(2)}) collective-permute-start(f32[4,64,128]{2,1,0:T(8,128)S(1)} %get-tuple-element.21), channel_id=1, source_target_pairs={{0,4},{1,5},{2,6},{3,7},{4,8},{5,9},{6,10},{7,11},{8,12},{9,13},{1... | collective-permute-start | bytes 393224 | tf_op jit(solution)/shard_map/ppermute | solution.py:212
  150.3 0.0 collective-permute-start.15
  150.3 2.6 %collective-permute-start.16 = (f32[4,64,128]{2,1,0:T(8,128)S(1)}, f32[4,64,128]{2,1,0:T(8,128)S(1)}, u32[]{:S(2)}, u32[]{:S(2)}) collective-permute-start(f32[4,64,128]{2,1,0:T(8,128)S(1)} %get-tuple-element.23), channel_id=1, source_target_pairs={{0,8},{1,9},{2,10},{3,11},{4,12},{5,13},{6,14},{7,15},{8,0},{9,1},... | collective-permute-start | bytes 393224 | tf_op jit(solution)/shard_map/ppermute | solution.py:212
  152.9 3.9 %all-to-all-done.7 = f32[8,2,64,128]{3,2,1,0:T(8,128)S(1)} async-done(((f32[8,2,64,128]{3,2,1,0:T(8,128)}), f32[8,2,64,128]{3,2,1,0:T(8,128)S(1)}, u32[]{:S(2)}, u32[]{:S(2)}) %all-to-all-start.7) | async-done | bytes 524320 | tf_op jit(solution)/shard_map/all_to_all | solution.py:195
  156.9 6.6 %collective-permute-start.17 = (f32[64,128]{1,0:T(8,128)S(1)}, f32[64,128]{1,0:T(8,128)S(1)}, u32[]{:S(2)}, u32[]{:S(2)}) collective-permute-start(f32[64,128]{1,0:T(8,128)S(1)} %slice_bitcast_fusion), channel_id=1, source_target_pairs={{0,128},{16,144},{32,160},{48,176},{64,192},{80,208},{96,224},{112... | collective-permute-start | bytes 98312 | tf_op jit(solution)/shard_map/ppermute | solution.py:208
  163.4 0.0 collective-permute-done.14
  163.4 0.0 collective-permute-done.15
  163.4 0.0 collective-permute-done.16
  163.4 0.7 add_add_fusion
  164.1 3.9 %all-to-all-start.6 = ((f32[4,64,128]{2,1,0:T(8,128)}), f32[4,64,128]{2,1,0:T(8,128)S(1)}, u32[]{:S(2)}, u32[]{:S(2)}) async-start(f32[4,64,128]{2,1,0:T(8,128)} %add_add_fusion), calls=%async_computation.6 | async-start | bytes 262144 | tf_op jit(solution)/shard_map/all_to_all | solution.py:195
  168.0 0.0 collective-permute-done.17
  168.0 4.8 %collective-permute-start.18 = (f32[64,128]{1,0:T(8,128)S(1)}, f32[64,128]{1,0:T(8,128)S(1)}, u32[]{:S(2)}, u32[]{:S(2)}) collective-permute-start(f32[64,128]{1,0:T(8,128)S(1)} %fusion), channel_id=1, source_target_pairs={{0,0},{1,16},{2,32},{3,48},{4,64},{5,80},{6,96},{7,112},{8,128},{9... | collective-permute-start | bytes 98312 | tf_op jit(solution)/shard_map/ppermute | solution.py:204
  172.9 1.1 all-to-all-done.6
  174.0 8.3 %collective-permute-done.18 = f32[64,128]{1,0:T(8,128)S(1)} collective-permute-done((f32[64,128]{1,0:T(8,128)S(1)}, f32[64,128]{1,0:T(8,128)S(1)}, u32[]{:S(2)}, u32[]{:S(2)}) %collective-permute-start.18) | collective-permute-done | bytes 32800 | tf_op jit(solution)/shard_map/ppermute | solution.py:204
  182.3 0.6 add_multiply_fusion
  (12 shorter events, 0.1 us)
Async XLA Ops:
  1.4 28.5 %all-to-all-start = ((f32[4,64,128]{2,1,0:T(8,128)}), f32[4,64,128]{2,1,0:T(8,128)S(1)}, u32[]{:S(2)}, u32[]{:S(2)}) async-start(f32[4,64,128]{2,1,0:T(8,128)} %broadcast_in_dim.12), calls=%async_computation | async-start | bytes 262144 | tf_op jit(solution)/shard_map/all_to_all | solution.py:195
  7.3 14.4 %collective-permute-start.3 = (f32[64,128]{1,0:T(8,128)}, f32[64,128]{1,0:T(8,128)S(1)}, u32[]{:S(2)}, u32[]{:S(2)}) collective-permute-start(f32[64,128]{1,0:T(8,128)} %param.2), channel_id=1, source_target_pairs={{0,0},{1,16},{2,32},{3,48},{4,64},{5,80},{6,96},{7,112},{8,128},{9... | collective-permute-start | bytes 98312 | tf_op jit(solution)/shard_map/ppermute | solution.py:204
  21.7 8.2 %collective-permute-start.4 = (f32[64,128]{1,0:T(8,128)S(1)}, f32[64,128]{1,0:T(8,128)S(1)}, u32[]{:S(2)}, u32[]{:S(2)}) collective-permute-start(f32[64,128]{1,0:T(8,128)S(1)} %collective-permute-done.3), channel_id=1, source_target_pairs={{0,128},{16,144},{32,160},{48,176},{64,192},{80,208},{96,224},{112... | collective-permute-start | bytes 98312 | tf_op jit(solution)/shard_map/ppermute | solution.py:208
  30.8 13.8 %all-to-all-start.1 = ((f32[8,2,64,128]{3,2,1,0:T(8,128)}), f32[8,2,64,128]{3,2,1,0:T(8,128)S(1)}, u32[]{:S(2)}, u32[]{:S(2)}) async-start(f32[8,2,64,128]{3,2,1,0:T(8,128)} %broadcast_in_dim.13), calls=%async_computation.1 | async-start | bytes 1048576 | tf_op jit(solution)/shard_map/all_to_all | solution.py:195
  34.3 8.0 %collective-permute-start.2 = (f32[4,64,128]{2,1,0:T(8,128)S(1)}, f32[4,64,128]{2,1,0:T(8,128)S(1)}, u32[]{:S(2)}, u32[]{:S(2)}) collective-permute-start(f32[4,64,128]{2,1,0:T(8,128)S(1)} %all-to-all-done.refs_0_), channel_id=1, source_target_pairs={{0,8},{1,9},{2,10},{3,11},{4,12},{5,13},{6,14},{7,15},{8,0},{9,1},... | collective-permute-start | bytes 393224 | tf_op jit(solution)/shard_map/ppermute | solution.py:212
  34.4 9.9 %collective-permute-start.1 = (f32[4,64,128]{2,1,0:T(8,128)S(1)}, f32[4,64,128]{2,1,0:T(8,128)S(1)}, u32[]{:S(2)}, u32[]{:S(2)}) collective-permute-start(f32[4,64,128]{2,1,0:T(8,128)S(1)} %all-to-all-done.refs_0_), channel_id=1, source_target_pairs={{0,12},{1,13},{2,14},{3,15},{4,0},{5,1},{6,2},{7,3},{8,4},{9,5},{1... | collective-permute-start | bytes 393224 | tf_op jit(solution)/shard_map/ppermute | solution.py:212
  35.0 9.3 %collective-permute-start = (f32[4,64,128]{2,1,0:T(8,128)S(1)}, f32[4,64,128]{2,1,0:T(8,128)S(1)}, u32[]{:S(2)}, u32[]{:S(2)}) collective-permute-start(f32[4,64,128]{2,1,0:T(8,128)S(1)} %all-to-all-done.refs_0_), channel_id=1, source_target_pairs={{0,4},{1,5},{2,6},{3,7},{4,8},{5,9},{6,10},{7,11},{8,12},{9,13},{1... | collective-permute-start | bytes 393224 | tf_op jit(solution)/shard_map/ppermute | solution.py:212
  57.0 18.6 %all-to-all-start.3 = ((f32[8,2,64,128]{3,2,1,0:T(8,128)}), f32[8,2,64,128]{3,2,1,0:T(8,128)S(1)}, u32[]{:S(2)}, u32[]{:S(2)}) async-start(f32[8,2,64,128]{3,2,1,0:T(8,128)} %get-tuple-element.19), calls=%async_computation.3 | async-start | bytes 1048576 | tf_op jit(solution)/shard_map/all_to_all | solution.py:195
  61.2 7.3 %collective-permute-start.5 = (f32[4,64,128]{2,1,0:T(8,128)S(1)}, f32[4,64,128]{2,1,0:T(8,128)S(1)}, u32[]{:S(2)}, u32[]{:S(2)}) collective-permute-start(f32[4,64,128]{2,1,0:T(8,128)S(1)} %get-tuple-element.16), channel_id=1, source_target_pairs={{0,4},{1,5},{2,6},{3,7},{4,8},{5,9},{6,10},{7,11},{8,12},{9,13},{1... | collective-permute-start | bytes 393224 | tf_op jit(solution)/shard_map/ppermute | solution.py:212
  64.9 6.8 %collective-permute-start.6 = (f32[4,64,128]{2,1,0:T(8,128)S(1)}, f32[4,64,128]{2,1,0:T(8,128)S(1)}, u32[]{:S(2)}, u32[]{:S(2)}) collective-permute-start(f32[4,64,128]{2,1,0:T(8,128)S(1)} %get-tuple-element.17), channel_id=1, source_target_pairs={{0,12},{1,13},{2,14},{3,15},{4,0},{5,1},{6,2},{7,3},{8,4},{9,5},{1... | collective-permute-start | bytes 393224 | tf_op jit(solution)/shard_map/ppermute | solution.py:212
  64.9 10.0 %collective-permute-start.7 = (f32[4,64,128]{2,1,0:T(8,128)S(1)}, f32[4,64,128]{2,1,0:T(8,128)S(1)}, u32[]{:S(2)}, u32[]{:S(2)}) collective-permute-start(f32[4,64,128]{2,1,0:T(8,128)S(1)} %get-tuple-element.18), channel_id=1, source_target_pairs={{0,8},{1,9},{2,10},{3,11},{4,12},{5,13},{6,14},{7,15},{8,0},{9,1},... | collective-permute-start | bytes 393224 | tf_op jit(solution)/shard_map/ppermute | solution.py:212
  75.6 9.7 %all-to-all-start.2 = ((f32[4,64,128]{2,1,0:T(8,128)}), f32[4,64,128]{2,1,0:T(8,128)S(1)}, u32[]{:S(2)}, u32[]{:S(2)}) async-start(f32[4,64,128]{2,1,0:T(8,128)} %add_add_fusion.1), calls=%async_computation.2 | async-start | bytes 262144 | tf_op jit(solution)/shard_map/all_to_all | solution.py:195
  79.4 7.9 %collective-permute-start.8 = (f32[64,128]{1,0:T(8,128)S(1)}, f32[64,128]{1,0:T(8,128)S(1)}, u32[]{:S(2)}, u32[]{:S(2)}) collective-permute-start(f32[64,128]{1,0:T(8,128)S(1)} %slice_bitcast_fusion.4), channel_id=1, source_target_pairs={{0,128},{16,144},{32,160},{48,176},{64,192},{80,208},{96,224},{112... | collective-permute-start | bytes 98312 | tf_op jit(solution)/shard_map/ppermute | solution.py:208
  87.3 15.9 %collective-permute-start.9 = (f32[2,64,128]{2,1,0:T(8,128)S(1)}, f32[2,64,128]{2,1,0:T(8,128)S(1)}, u32[]{:S(2)}, u32[]{:S(2)}) collective-permute-start(f32[2,64,128]{2,1,0:T(8,128)S(1)} %pad_maximum_fusion.1), channel_id=1, source_target_pairs={{0,0},{1,16},{2,32},{3,48},{4,64},{5,80},{6,96},{7,112},{8,128},{9... | collective-permute-start | bytes 196616 | tf_op jit(solution)/shard_map/ppermute | solution.py:204
  103.9 11.2 %all-to-all-start.4 = ((f32[4,64,128]{2,1,0:T(8,128)}), f32[4,64,128]{2,1,0:T(8,128)S(1)}, u32[]{:S(2)}, u32[]{:S(2)}) async-start(f32[4,64,128]{2,1,0:T(8,128)} %broadcast_in_dim.14), calls=%async_computation.4 | async-start | bytes 262144 | tf_op jit(solution)/shard_map/all_to_all | solution.py:195
  107.2 7.9 %collective-permute-start.13 = (f32[64,128]{1,0:T(8,128)S(1)}, f32[64,128]{1,0:T(8,128)S(1)}, u32[]{:S(2)}, u32[]{:S(2)}) collective-permute-start(f32[64,128]{1,0:T(8,128)S(1)} %get-tuple-element.25), channel_id=1, source_target_pairs={{0,128},{16,144},{32,160},{48,176},{64,192},{80,208},{96,224},{112... | collective-permute-start | bytes 98312 | tf_op jit(solution)/shard_map/ppermute | solution.py:208
  116.0 13.9 %all-to-all-start.5 = ((f32[8,2,64,128]{3,2,1,0:T(8,128)}), f32[8,2,64,128]{3,2,1,0:T(8,128)S(1)}, u32[]{:S(2)}, u32[]{:S(2)}) async-start(f32[8,2,64,128]{3,2,1,0:T(8,128)} %broadcast_in_dim.15), calls=%async_computation.5 | async-start | bytes 1048576 | tf_op jit(solution)/shard_map/all_to_all | solution.py:195
  119.6 7.9 %collective-permute-start.12 = (f32[4,64,128]{2,1,0:T(8,128)S(1)}, f32[4,64,128]{2,1,0:T(8,128)S(1)}, u32[]{:S(2)}, u32[]{:S(2)}) collective-permute-start(f32[4,64,128]{2,1,0:T(8,128)S(1)} %all-to-all-done.4.refs_0_), channel_id=1, source_target_pairs={{0,8},{1,9},{2,10},{3,11},{4,12},{5,13},{6,14},{7,15},{8,0},{9,1},... | collective-permute-start | bytes 393224 | tf_op jit(solution)/shard_map/ppermute | solution.py:212
  119.6 9.9 %collective-permute-start.11 = (f32[4,64,128]{2,1,0:T(8,128)S(1)}, f32[4,64,128]{2,1,0:T(8,128)S(1)}, u32[]{:S(2)}, u32[]{:S(2)}) collective-permute-start(f32[4,64,128]{2,1,0:T(8,128)S(1)} %all-to-all-done.4.refs_0_), channel_id=1, source_target_pairs={{0,12},{1,13},{2,14},{3,15},{4,0},{5,1},{6,2},{7,3},{8,4},{9,5},{1... | collective-permute-start | bytes 393224 | tf_op jit(solution)/shard_map/ppermute | solution.py:212
  120.9 8.6 %collective-permute-start.10 = (f32[4,64,128]{2,1,0:T(8,128)S(1)}, f32[4,64,128]{2,1,0:T(8,128)S(1)}, u32[]{:S(2)}, u32[]{:S(2)}) collective-permute-start(f32[4,64,128]{2,1,0:T(8,128)S(1)} %all-to-all-done.4.refs_0_), channel_id=1, source_target_pairs={{0,4},{1,5},{2,6},{3,7},{4,8},{5,9},{6,10},{7,11},{8,12},{9,13},{1... | collective-permute-start | bytes 393224 | tf_op jit(solution)/shard_map/ppermute | solution.py:212
  142.4 14.4 %all-to-all-start.7 = ((f32[8,2,64,128]{3,2,1,0:T(8,128)}), f32[8,2,64,128]{3,2,1,0:T(8,128)S(1)}, u32[]{:S(2)}, u32[]{:S(2)}) async-start(f32[8,2,64,128]{3,2,1,0:T(8,128)} %get-tuple-element.24), calls=%async_computation.7 | async-start | bytes 1048576 | tf_op jit(solution)/shard_map/all_to_all | solution.py:195
  146.5 17.0 %collective-permute-start.14 = (f32[4,64,128]{2,1,0:T(8,128)S(1)}, f32[4,64,128]{2,1,0:T(8,128)S(1)}, u32[]{:S(2)}, u32[]{:S(2)}) collective-permute-start(f32[4,64,128]{2,1,0:T(8,128)S(1)} %get-tuple-element.21), channel_id=1, source_target_pairs={{0,4},{1,5},{2,6},{3,7},{4,8},{5,9},{6,10},{7,11},{8,12},{9,13},{1... | collective-permute-start | bytes 393224 | tf_op jit(solution)/shard_map/ppermute | solution.py:212
  150.3 13.1 %collective-permute-start.15 = (f32[4,64,128]{2,1,0:T(8,128)S(1)}, f32[4,64,128]{2,1,0:T(8,128)S(1)}, u32[]{:S(2)}, u32[]{:S(2)}) collective-permute-start(f32[4,64,128]{2,1,0:T(8,128)S(1)} %get-tuple-element.22), channel_id=1, source_target_pairs={{0,12},{1,13},{2,14},{3,15},{4,0},{5,1},{6,2},{7,3},{8,4},{9,5},{1... | collective-permute-start | bytes 393224 | tf_op jit(solution)/shard_map/ppermute | solution.py:212
  150.3 13.1 %collective-permute-start.16 = (f32[4,64,128]{2,1,0:T(8,128)S(1)}, f32[4,64,128]{2,1,0:T(8,128)S(1)}, u32[]{:S(2)}, u32[]{:S(2)}) collective-permute-start(f32[4,64,128]{2,1,0:T(8,128)S(1)} %get-tuple-element.23), channel_id=1, source_target_pairs={{0,8},{1,9},{2,10},{3,11},{4,12},{5,13},{6,14},{7,15},{8,0},{9,1},... | collective-permute-start | bytes 393224 | tf_op jit(solution)/shard_map/ppermute | solution.py:212
  156.9 11.2 %collective-permute-start.17 = (f32[64,128]{1,0:T(8,128)S(1)}, f32[64,128]{1,0:T(8,128)S(1)}, u32[]{:S(2)}, u32[]{:S(2)}) collective-permute-start(f32[64,128]{1,0:T(8,128)S(1)} %slice_bitcast_fusion), channel_id=1, source_target_pairs={{0,128},{16,144},{32,160},{48,176},{64,192},{80,208},{96,224},{112... | collective-permute-start | bytes 98312 | tf_op jit(solution)/shard_map/ppermute | solution.py:208
  164.1 9.8 %all-to-all-start.6 = ((f32[4,64,128]{2,1,0:T(8,128)}), f32[4,64,128]{2,1,0:T(8,128)S(1)}, u32[]{:S(2)}, u32[]{:S(2)}) async-start(f32[4,64,128]{2,1,0:T(8,128)} %add_add_fusion), calls=%async_computation.6 | async-start | bytes 262144 | tf_op jit(solution)/shard_map/all_to_all | solution.py:195
  168.0 14.2 %collective-permute-start.18 = (f32[64,128]{1,0:T(8,128)S(1)}, f32[64,128]{1,0:T(8,128)S(1)}, u32[]{:S(2)}, u32[]{:S(2)}) collective-permute-start(f32[64,128]{1,0:T(8,128)S(1)} %fusion), channel_id=1, source_target_pairs={{0,0},{1,16},{2,32},{3,48},{4,64},{5,80},{6,96},{7,112},{8,128},{9... | collective-permute-start | bytes 98312 | tf_op jit(solution)/shard_map/ppermute | solution.py:204
